TPU v7x, 32 devices: a whole 2x2x4 slice. The times are simulated.
32 devices in a mesh: phi: 4 (over y, core), eta: 8 (over z, x).
Axes of the slice: x: 2, y: 2, z: 4, core: 2. Of those that a mesh axis runs over, the one named last changes fastest.
Arguments:
- edges: bfloat16 [65536, 128], P(('phi', 'eta')), may hold values from -6 to 6
- cotangent: bfloat16 [65536, 128], P(('phi', 'eta')), may hold values from -6 to 6
- send_rows: int32 [32, 32, 32], P(('phi', 'eta')), may hold values from 0 to 2047
- send_count: int32 [32, 32], P(('phi', 'eta')), may hold values from 1 to 32, as said below
- trip_local: int32 [262144], P(('phi', 'eta')), may hold values from 0 to 2047
- trip_remote: int32 [262144], P(('phi', 'eta')), may hold values from 0 to 1023, as said below
- w_first: bfloat16 [384, 256], replicated, may hold values from -0.3125 to 0.3125
- bias_first: float32 [256], replicated, may hold values from -4 to 4
- w_second: bfloat16 [256, 128], replicated, may hold values from -0.375 to 0.375
Outputs:
- new_edges: bfloat16 [65536, 128], P(('phi', 'eta'))
- edge_grad: bfloat16 [65536, 128], P(('phi', 'eta'))
- grad_first: float32 [384, 256], replicated
- grad_bias: float32 [256], replicated
- grad_second: float32 [256, 128], replicated
Inputs may be any that keep to these rules, and one draw needn't show every extreme that they name: `send_count`: some destination device has every slot live from every source. `trip_remote`: each triplet names a live slot of a source device toward its own owner.
All inputs are finite; a program needn't handle non-finite values.
Results may differ from a plain program's by a relative error of at most 0.0053.
Values may be sent and summed in bfloat16 or wider, within the bound.
A program may use at most 128 MiB of HBM per device.

v0:
```python
import jax
import jax.numpy as jnp
from jax import lax
from jax.sharding import PartitionSpec as P


def silu_slope(pre):
    sig = jax.nn.sigmoid(pre)
    return sig * (1.0 + pre * (1.0 - sig))


def local(
    edges, cotangent, send_rows, send_count, trip_local, trip_remote, w_first, bias_first, w_second
):
    width = edges.shape[1]
    local_edges = edges.shape[0]
    n_phi = lax.axis_size("phi")
    n_eta = lax.axis_size("eta")
    ndev = n_phi * n_eta
    slots_per = send_rows.shape[2]
    rows = send_rows[0]
    live = jnp.arange(slots_per, dtype=jnp.int32)[None, :] < send_count[0][:, None]
    zero = jnp.zeros((), jnp.bfloat16)
    stacked = jnp.stack([edges, cotangent], axis=1)
    outgoing = jnp.where(live[:, :, None, None], stacked[rows], zero)
    arrived = lax.all_to_all(outgoing, ("phi", "eta"), split_axis=0, concat_axis=0, tiled=True)
    arrived = arrived.reshape(ndev * slots_per, 2, width)
    inner = edges[trip_local]
    inner_cot = cotangent[trip_local]
    outer_pair = arrived[trip_remote]
    outer = outer_pair[:, 0, :]
    outer_cot = outer_pair[:, 1, :]
    inner_f = inner.astype(jnp.float32)
    outer_f = outer.astype(jnp.float32)
    prod = (inner_f * outer_f).astype(jnp.bfloat16)
    joined = jnp.concatenate([inner, outer, prod], axis=1)
    pre = jnp.dot(joined, w_first, preferred_element_type=jnp.float32) + bias_first
    hidden = jax.nn.silu(pre).astype(jnp.bfloat16)
    message = jnp.dot(hidden, w_second, preferred_element_type=jnp.float32)
    dmsg = (inner_cot.astype(jnp.float32) + outer_cot.astype(jnp.float32)).astype(jnp.bfloat16)
    dpre = jnp.dot(dmsg, w_second.T, preferred_element_type=jnp.float32) * silu_slope(pre)
    dpre_b = dpre.astype(jnp.bfloat16)
    dx = jnp.dot(dpre_b, w_first.T, preferred_element_type=jnp.float32)
    d_inner = dx[:, :width] + dx[:, 2 * width :] * outer_f
    d_outer = dx[:, width : 2 * width] + dx[:, 2 * width :] * inner_f
    slot_msg = jax.ops.segment_sum(message, trip_remote, ndev * slots_per)
    slot_grad = jax.ops.segment_sum(d_outer, trip_remote, ndev * slots_per)
    slot_sums = (
        jnp.stack([slot_msg, slot_grad], axis=1)
        .astype(jnp.bfloat16)
        .reshape(ndev, slots_per, 2, width)
    )
    returned = lax.all_to_all(slot_sums, ("phi", "eta"), split_axis=0, concat_axis=0, tiled=True)
    returned = jnp.where(live[:, :, None, None], returned, zero)
    grad_second = jnp.dot(hidden.T, dmsg, preferred_element_type=jnp.float32)
    grad_first = jnp.dot(joined.T, dpre_b, preferred_element_type=jnp.float32)
    grad_bias = jnp.sum(dpre, axis=0)
    grad_first, grad_bias, grad_second = lax.psum(
        (grad_first, grad_bias, grad_second), ("phi", "eta")
    )
    local_msg = jax.ops.segment_sum(message, trip_local, local_edges)
    local_grad = jax.ops.segment_sum(d_inner, trip_local, local_edges)
    flat_rows = rows.reshape(-1)
    local_msg = local_msg.at[flat_rows].add(
        returned[:, :, 0, :].astype(jnp.float32).reshape(-1, width)
    )
    local_grad = local_grad.at[flat_rows].add(
        returned[:, :, 1, :].astype(jnp.float32).reshape(-1, width)
    )
    new_edges = (edges.astype(jnp.float32) + local_msg).astype(jnp.bfloat16)
    edge_grad = (cotangent.astype(jnp.float32) + local_grad).astype(jnp.bfloat16)
    return (new_edges, edge_grad, grad_first, grad_bias, grad_second)


def solution(mesh):
    in_specs = (
        P(("phi", "eta"), None),
        P(("phi", "eta"), None),
        P(("phi", "eta"), None, None),
        P(("phi", "eta"), None),
        P(("phi", "eta")),
        P(("phi", "eta")),
        P(),
        P(),
        P(),
    )
    out_specs = (P(("phi", "eta"), None), P(("phi", "eta"), None), P(), P(), P())
    return jax.shard_map(local, mesh=mesh, in_specs=in_specs, out_specs=out_specs, check_vma=False)
```

profile of v0, /device:TPU:0, one launch (start us, length us, event | category | flops | bytes accessed | tf_op | source)
XLA Modules:
  0.0 520.3 jit_solution(7421459561959832188)
XLA Ops:
  7.2 0.0 copy-start
  7.2 0.8 iota_compare_fusion
  8.0 0.7 compare_select_fusion.2
  8.7 0.1 reshape.125
  8.8 1.8 copy.21
  10.6 0.0 copy-start.11
  10.6 0.0 copy-start.2
  10.6 1.9 copy.20
  12.4 0.0 copy-start.3
  12.5 0.0 copy-start.9
  12.5 2.4 pad_maximum_fusion.3
  14.9 3.7 gather_fusion.1
  18.6 1.0 copy_select_fusion
  19.6 7.3 %all-to-all-start = ((bf16[32,32,2,128]{3,1,2,0:T(8,128)(2,1)}), bf16[32,32,2,128]{3,1,2,0:T(8,128)(2,1)S(1)}, u32[]{:S(2)}, u32[]{:S(2)}) async-start(bf16[32,32,2,128]{3,1,2,0:T(8,128)(2,1)} %copy_select_fusion), calls=%async_computation | async-start | bytes 1048576 | tf_op jit(solution)/shard_map/all_to_all | solution.py:26
  26.9 0.0 copy-done.11
  26.9 0.1 reshape_squeeze.3
  27.0 0.0 copy-done.2
  27.0 0.1 convert_element_type.55
  27.1 0.0 copy-done.3
  27.1 1.1 convert_element_type.68
  28.2 0.0 copy-done.9
  28.2 29.2 %gather_fusion = bf16[8192,128]{1,0:T(8,128)(2,1)} fusion(bf16[2048,128]{1,0:T(8,128)(2,1)S(1)} %copy-done.2, s32[8192]{0:T(1024)S(1)} %fusion.22), kind=kCustom, calls=%fused_computation | custom fusion | bytes 4227072 | tf_op jit(solution)/shard_map/gather | solution.py:28
  57.4 29.2 %gather_fusion.3 = bf16[8192,128]{1,0:T(8,128)(2,1)} fusion(bf16[2048,128]{1,0:T(8,128)(2,1)S(1)} %copy-done.3, s32[8192]{0:T(1024)S(1)} %fusion.22), kind=kCustom, calls=%fused_computation.3 | custom fusion | bytes 4227072 | tf_op jit(solution)/shard_map/gather | solution.py:29
  86.6 0.0 copy-done.12
  86.7 0.0 all-to-all-done
  86.7 0.5 copy.23
  87.2 53.3 %gather_fusion.2 = bf16[8192,2,128]{2,1,0:T(2,128)(2,1)} fusion(bf16[1024,2,128]{2,1,0:T(2,128)(2,1)S(1)} %bitcast.30, s32[8192]{0:T(1024)S(1)} %fusion.23), kind=kCustom, calls=%fused_computation.2 | custom fusion | bytes 8421376 | tf_op jit(solution)/shard_map/gather | solution.py:30
  140.5 9.5 %slice_convert_fusion = (f32[8192,1,128]{2,1,0:T(1,128)}, bf16[8192,1,128]{2,1,0:T(2,128)(2,1)S(1)}) fusion(bf16[8192,2,128]{2,1,0:T(2,128)(2,1)} %gather_fusion.2), kind=kLoop, calls=%fused_computation.25 | loop fusion | flops 1048576 | bytes 10485760 | tf_op jit(solution)/shard_map/convert_element_type | solution.py:40
  150.0 0.0 copy-done.5
  150.0 0.8 fusion.3
  150.9 0.0 copy-start.6
  150.9 0.0 copy-start.8
  150.9 0.0 copy-done
  150.9 0.0 copy-done.13
  150.9 0.0 copy-start.10
  150.9 5.2 %multiply_convert_fusion = (bf16[8192,256]{1,0:T(8,128)(2,1)S(1)}, f32[8192,256]{1,0:T(8,128)}) fusion(f32[256]{0:T(256)S(1)} %copy-done.13, bf16[384,256]{1,0:T(8,128)(2,1)S(1)} %copy-done, bf16[8192,128]{1,0:T(8,128)(2,1)S(1)} %get-tuple-element.7, bf16[8192,128]{1,0:T(8,128)(2,1)S(1)} %get-tuple-element.8, bf16[8192,128]{1,0:T(8,128)(2,1)S(1)} %copy-done.5), kind=kOutput, calls=%fused_computation.12 | convolution fusion | flops 1642070016 | bytes 19072000 | tf_op jit(solution)/shard_map/dot_general | solution.py:37
  156.1 2.0 copy-done.4
  158.1 3.2 fusion.29
  161.3 45.1 %scatter_custom_fusion.1 = f32[1024,128]{1,0:T(8,128)} fusion(s32[8192]{0:T(1024)S(1)} %copy-done.12, f32[8192,128]{1,0:T(8,128)} %fusion.29, f32[]{:T(128)} %constant.11.clone.1), kind=kCustom, calls=%fused_computation.43 | custom fusion | flops 1048576 | bytes 524800 | tf_op jit(solution)/shard_map/scatter-add | solution.py:46
  206.4 1.8 convert.11
  208.2 7.9 %fusion.28 = (f32[256]{0:T(256)S(1)}, bf16[8192,256]{1,0:T(8,128)(2,1)S(1)}) fusion(f32[8192,256]{1,0:T(8,128)} %get-tuple-element.14, bf16[256,128]{1,0:T(8,128)(2,1)S(1)} %copy-done.10, f32[8192,128]{1,0:T(8,128)} %bitcast.31, bf16[8192,128]{1,0:T(8,128)(2,1)} %gather_fusion.3), kind=kOutput, calls=%fused_computation.57 | convolution fusion | flops 560987904 | bytes 18940928 | tf_op jit(solution)/shard_map/dot_general | solution.py:41
  216.1 1.9 copy-done.7
  218.0 6.9 %fusion.13 = f32[8192,384]{1,0:T(8,128)} fusion(bf16[384,256]{1,0:T(8,128)(2,1)S(1)} %copy-done, bf16[8192,256]{1,0:T(8,128)(2,1)S(1)} %get-tuple-element.16), kind=kOutput, calls=%fused_computation.32 | convolution fusion | flops 1610612736 | bytes 16973824 | tf_op jit(solution)/shard_map/dot_general | solution.py:43
  224.9 45.7 %scatter_custom_fusion.2 = f32[1024,128]{1,0:T(8,128)} fusion(s32[8192]{0:T(1024)S(1)} %copy-done.12, bf16[8192,128]{1,0:T(8,128)(2,1)S(1)} %copy-done.5, f32[8192,384]{1,0:T(8,128)} %fusion.13, f32[]{:T(128)} %constant.11.clone.1), kind=kCustom, calls=%fused_computation.19 | custom fusion | flops 4194304 | bytes 11010560 | tf_op jit(solution)/shard_map/scatter-add | solution.py:47
  270.7 1.1 convert.12
  271.7 1.0 pad_maximum_fusion.4
  272.8 0.9 copy.25
  273.6 5.9 %all-to-all-start.1 = ((bf16[32,32,2,128]{3,1,2,0:T(8,128)(2,1)}), bf16[32,32,2,128]{3,1,2,0:T(8,128)(2,1)}, u32[]{:S(2)}, u32[]{:S(2)}) async-start(bf16[32,32,2,128]{3,1,2,0:T(8,128)(2,1)} %copy.25), calls=%async_computation.1 | async-start | bytes 1048576 | tf_op jit(solution)/shard_map/all_to_all | solution.py:53
  279.6 0.0 all-reduce.3.cloned.1.call-start
  279.6 6.0 %fusion.26 = f32[256,128]{1,0:T(8,128)} fusion(bf16[8192,256]{1,0:T(8,128)(2,1)} %copy-done.4, f32[8192,128]{1,0:T(8,128)} %bitcast.32, bf16[8192,128]{1,0:T(8,128)(2,1)} %gather_fusion.3), kind=kOutput, calls=%fused_computation.55 | convolution fusion | flops 540016640 | bytes 10616832 | tf_op jit(solution)/shard_map/dot_general | solution.py:55
  285.6 44.7 %scatter_fusion = f32[2048,128]{1,0:T(8,128)S(1)} fusion(f32[2048,128]{1,0:T(8,128)S(1)} %convert_element_type.55, s32[8192]{0:T(1024)S(1)} %copy-done.9, f32[8192,128]{1,0:T(8,128)} %fusion.29), kind=kCustom, calls=%fused_computation.4 | custom fusion | flops 1048576 | bytes 12615680 | tf_op jit(solution)/shard_map/scatter-add | solution.py:61
  330.3 42.8 %scatter_custom_fusion.4 = f32[2048,128]{1,0:T(8,128)} fusion(f32[2048,128]{1,0:T(8,128)} %convert_element_type.68, s32[8192]{0:T(1024)S(1)} %copy-done.9, bf16[8192,128]{1,0:T(8,128)(2,1)} %copy-done.6, f32[8192,384]{1,0:T(8,128)} %fusion.13), kind=kCustom, calls=%fused_computation.22 | custom fusion | flops 4194304 | bytes 11534336 | tf_op jit(solution)/shard_map/scatter-add | solution.py:62
  373.2 6.0 %fusion.11 = f32[384,256]{1,0:T(8,128)} fusion(bf16[8192,128]{1,0:T(8,128)(2,1)} %copy-done.8, bf16[8192,128]{1,0:T(8,128)(2,1)} %copy-done.6, bf16[8192,128]{1,0:T(8,128)(2,1)S(1)} %copy-done.5, bf16[8192,256]{1,0:T(8,128)(2,1)} %copy-done.7), kind=kOutput, calls=%fused_computation.29 | convolution fusion | flops 1629487104 | bytes 10878976 | tf_op jit(solution)/shard_map/dot_general | solution.py:56
  379.2 0.0 all-reduce.3.cloned.1.call-update
  379.2 40.6 %psum.22 = f32[256]{0:T(256)} all-reduce(f32[256]{0:T(256)S(1)} %get-tuple-element.15), channel_id=1, replica_groups=mesh['phi'=4,'eta'=8] {'phi','eta'}, use_global_device_ids=true, to_apply=%region_8.9 | all-reduce | flops 256 | bytes 2048 | tf_op jit(solution)/shard_map/psum | solution.py:58
  419.8 0.0 all-to-all-done.1
  419.8 1.3 broadcast_select_fusion
  421.1 7.7 %scatter_custom_fusion.5 = f32[2048,128]{1,0:T(8,128)} fusion(f32[2048,128]{1,0:T(8,128)} %scatter_custom_fusion.4, s32[1024]{0:T(1024)S(1)} %bitcast.38, bf16[1024,128]{1,0:T(8,128)(2,1)S(1)} %bitcast.36), kind=kCustom, calls=%fused_computation.36 | custom fusion | flops 262144 | bytes 1310720 | tf_op jit(solution)/shard_map/scatter-add | solution.py:67
  428.8 2.1 convert_element_type.71
  430.9 6.5 %scatter_custom_fusion.3 = f32[2048,128]{1,0:T(8,128)S(1)} fusion(f32[2048,128]{1,0:T(8,128)S(1)} %scatter_fusion, s32[1024]{0:T(1024)S(1)} %bitcast.39, bf16[1024,128]{1,0:T(8,128)(2,1)S(1)} %bitcast.35), kind=kCustom, calls=%fused_computation.38 | custom fusion | flops 262144 | bytes 1310720 | tf_op jit(solution)/shard_map/scatter-add | solution.py:64
  437.3 0.8 convert_element_type.67
  438.2 71.9 %all-reduce.3.cloned.1.call-done = (f32[384,256]{1,0:T(8,128)}, f32[256,128]{1,0:T(8,128)}) async-done(((f32[384,256]{1,0:T(8,128)}, f32[256,128]{1,0:T(8,128)}), (f32[384,256]{1,0:T(8,128)}, f32[256,128]{1,0:T(8,128)})) %all-reduce.3.cloned.1.call-update) | async-done | bytes 524304 | tf_op jit(solution)/shard_map/psum | solution.py:58
  510.1 1.8 copy.36
  511.9 1.6 copy.37
  (15 shorter events, 0.1 us)
Async XLA Ops:
  7.2 143.7 %copy-start = (bf16[384,256]{1,0:T(8,128)(2,1)S(1)}, bf16[384,256]{1,0:T(8,128)(2,1)}, u32[]{:S(2)}) copy-start(bf16[384,256]{1,0:T(8,128)(2,1)} %param.15) | copy-start | bytes 589828
  10.6 16.4 %copy-start.11 = (s32[1,32,32]{2,1,0:T(8,128)S(1)}, s32[1,32,32]{2,1,0:T(8,128)}, u32[]{:S(2)}) copy-start(s32[1,32,32]{2,1,0:T(8,128)} %param.11) | copy-start | bytes 12292
  10.6 16.5 %copy-start.2 = (bf16[2048,128]{1,0:T(8,128)(2,1)S(1)}, bf16[2048,128]{1,0:T(8,128)(2,1)}, u32[]{:S(2)}) copy-start(bf16[2048,128]{1,0:T(8,128)(2,1)} %param.9) | copy-start | bytes 1572868
  12.4 14.7 %copy-start.3 = (bf16[2048,128]{1,0:T(8,128)(2,1)S(1)}, bf16[2048,128]{1,0:T(8,128)(2,1)}, u32[]{:S(2)}) copy-start(bf16[2048,128]{1,0:T(8,128)(2,1)} %param.10) | copy-start | bytes 1572868
  12.5 15.7 %copy-start.9 = (s32[8192]{0:T(1024)S(1)}, s32[8192]{0:T(1024)}, u32[]{:S(2)}) copy-start(s32[8192]{0:T(1024)} %param.13) | copy-start | bytes 98308
  19.6 67.1 %all-to-all-start = ((bf16[32,32,2,128]{3,1,2,0:T(8,128)(2,1)}), bf16[32,32,2,128]{3,1,2,0:T(8,128)(2,1)S(1)}, u32[]{:S(2)}, u32[]{:S(2)}) async-start(bf16[32,32,2,128]{3,1,2,0:T(8,128)(2,1)} %copy_select_fusion), calls=%async_computation | async-start | bytes 1048576 | tf_op jit(solution)/shard_map/all_to_all | solution.py:26
  57.4 29.2 %copy-start.12 = (s32[8192]{0:T(1024)S(1)}, s32[8192]{0:T(1024)}, u32[]{:S(2)}) copy-start(s32[8192]{0:T(1024)} %param.14) | copy-start | bytes 98308
  140.5 9.5 %copy-start.5 = (bf16[8192,128]{1,0:T(8,128)(2,1)S(1)}, bf16[8192,128]{1,0:T(8,128)(2,1)}, u32[]{:S(2)}) copy-start(bf16[8192,128]{1,0:T(8,128)(2,1)} %gather_fusion) | copy-start | bytes 6291460
  150.0 0.9 copy-start.13
  150.9 5.3 %copy-start.6 = (bf16[8192,128]{1,0:T(8,128)(2,1)}, bf16[8192,128]{1,0:T(8,128)(2,1)S(1)}, u32[]{:S(2)}) copy-start(bf16[8192,128]{1,0:T(8,128)(2,1)S(1)} %get-tuple-element.8) | copy-start | bytes 6291460
  150.9 5.3 %copy-start.8 = (bf16[8192,128]{1,0:T(8,128)(2,1)}, bf16[8192,128]{1,0:T(8,128)(2,1)S(1)}, u32[]{:S(2)}) copy-start(bf16[8192,128]{1,0:T(8,128)(2,1)S(1)} %get-tuple-element.7) | copy-start | bytes 6291460
  150.9 7.2 %copy-start.10 = (bf16[256,128]{1,0:T(8,128)(2,1)S(1)}, bf16[256,128]{1,0:T(8,128)(2,1)}, u32[]{:S(2)}) copy-start(bf16[256,128]{1,0:T(8,128)(2,1)} %param.17) | copy-start | bytes 196612
  156.1 2.0 copy-start.4
  216.1 1.9 copy-start.7
  273.6 146.2 %all-to-all-start.1 = ((bf16[32,32,2,128]{3,1,2,0:T(8,128)(2,1)}), bf16[32,32,2,128]{3,1,2,0:T(8,128)(2,1)}, u32[]{:S(2)}, u32[]{:S(2)}) async-start(bf16[32,32,2,128]{3,1,2,0:T(8,128)(2,1)} %copy.25), calls=%async_computation.1 | async-start | bytes 1048576 | tf_op jit(solution)/shard_map/all_to_all | solution.py:53
  279.6 230.6 %all-reduce.3.cloned.1.call-start = ((), (), s32[]{:S(2)}) async-start(), calls=%async_computation.2 | async-start | bytes 1048576 | tf_op jit(solution)/shard_map/psum | solution.py:58
  419.8 93.7 %copy-start.1 = (bf16[384,256]{1,0:T(8,128)(2,1)S(1)}, bf16[384,256]{1,0:T(8,128)(2,1)}, u32[]{:S(2)}) copy-start(bf16[384,256]{1,0:T(8,128)(2,1)} %param.15) | copy-start | bytes 589828
Sparse Core Ops, SparseCore 0:
  379.3 130.7 all-reduce.2
where the time goes:
time: 521 us; the launch traced here: 520 us
  other arithmetic  217 us (42%)
  local copies, waits for them, and re-layouts  128 us (25%)
  waiting for transfers between devices  72 us (14%)
  blocking collectives  40.6 us (8%)
  matrix products  35.3 us (7%)
  between operations  14.3 us (3%)
  starting transfers between devices  13.3 us (3%)
    psum x1, waiting for transfers between devices, local(): lax.psum((grad_first, grad_bias, grad_second), ('phi', 'eta'))  71.9 us
    gather x1, local copies, waits for them, and re-layouts, local(): outer_pair = arrived[trip_remote]  53.3 us
    scatter-add x1, other arithmetic, local(): slot_grad = jax.ops.segment_sum(d_outer, trip_remote, ndev * slots_per)  45.7 us
    scatter-add x1, other arithmetic, local(): slot_msg = jax.ops.segment_sum(message, trip_remote, ndev * slots_per)  45.1 us
    scatter-add x1, other arithmetic, local(): local_msg = jax.ops.segment_sum(message, trip_local, local_edges)  44.7 us
    scatter-add x1, other arithmetic, local(): local_grad = jax.ops.segment_sum(d_inner, trip_local, local_edges)  42.8 us
    psum x1, blocking collectives, local(): lax.psum((grad_first, grad_bias, grad_second), ('phi', 'eta'))  40.6 us
    gather x1, local copies, waits for them, and re-layouts, local(): inner_cot = cotangent[trip_local]  29.2 us
  transfers between devices with their start and end apart: 3, of which 1 were waited for; matrix products, arithmetic and copies ran while one was open for 34% of the time, Pallas kernels for 0%

commit v1 on v0

v1 whole, which is shorter than its diff:
```python
import functools

import jax
import jax.numpy as jnp
from jax import lax
from jax.experimental import pallas as pl
from jax.experimental.pallas import tpu as pltpu
from jax.sharding import PartitionSpec as P

AXES = ("phi", "eta")
F32 = jnp.float32
BF16 = jnp.bfloat16
VMEM_LIMIT = 60 * 1024 * 1024


def dot(a, b):
    return jnp.dot(a, b, preferred_element_type=F32)


def dot_nt(a, b):
    return lax.dot_general(a, b, (((1,), (1,)), ((), ())), preferred_element_type=F32)


def dot_tn(a, b):
    return lax.dot_general(a, b, (((0,), (0,)), ((), ())), preferred_element_type=F32)


def pick_rows(idx, n):
    t = idx.shape[1]
    cols = jnp.broadcast_to(idx, (128, t)).T
    lane = lax.broadcasted_iota(jnp.int32, (t, 128), 1)
    parts = [jnp.where(cols - 128 * j == lane, 1.0, 0.0).astype(BF16) for j in range(n // 128)]
    return jnp.concatenate(parts, axis=1)


def pick_cols(idx, n, start=0):
    row = lax.broadcasted_iota(jnp.int32, (n, idx.shape[1]), 0)
    return jnp.where(row == idx - start, 1.0, 0.0).astype(BF16)


def send_kernel(rows_ref, edges_ref, cot_ref, out_ref, ec):
    width = edges_ref.shape[1]

    @pl.when(pl.program_id(0) == 0)
    def _():
        ec[:, :width] = edges_ref[...]
        ec[:, width:] = cot_ref[...]

    out_ref[...] = dot(pick_rows(rows_ref[0], ec.shape[0]), ec[...]).astype(BF16)


def main_kernel(
    loc_ref, rem_ref, edges_ref, cot_ref, arr_ref, w1_ref, b1_ref, w2_ref,
    local_ref, slot_ref, grad_ref, bias_ref,
    ec, acc_r, g1, g2,
):
    step = pl.program_id(0)
    width = edges_ref.shape[1]
    inner_n = edges_ref.shape[0]
    slots_n = arr_ref.shape[0]

    @pl.when(step == 0)
    def _():
        ec[:, :width] = edges_ref[...]
        ec[:, width:] = cot_ref[...]
        local_ref[...] = jnp.zeros_like(local_ref)
        acc_r[...] = jnp.zeros_like(acc_r)
        g1[...] = jnp.zeros_like(g1)
        g2[...] = jnp.zeros_like(g2)
        bias_ref[...] = jnp.zeros_like(bias_ref)

    loc = loc_ref[0]
    rem = rem_ref[0]
    near = dot(pick_rows(loc, inner_n), ec[...])
    far = dot(pick_rows(rem, slots_n), arr_ref[...])
    a = near[:, :width]
    b = far[:, :width]
    dm = (near[:, width:] + far[:, width:]).astype(BF16)
    x = jnp.concatenate([a.astype(BF16), b.astype(BF16), (a * b).astype(BF16)], axis=1)
    pre = dot(x, w1_ref[...]) + b1_ref[...]
    sig = 0.5 * jnp.tanh(0.5 * pre) + 0.5
    h = (pre * sig).astype(BF16)
    m = dot(h, w2_ref[...]).astype(BF16)
    dpre = dot_nt(dm, w2_ref[...]) * (sig * (1.0 + pre * (1.0 - sig)))
    dpre_b = dpre.astype(BF16)
    dx = dot_nt(dpre_b, w1_ref[...])
    dprod = dx[:, 2 * width :]
    da = (dx[:, :width] + dprod * b).astype(BF16)
    db = (dx[:, width : 2 * width] + dprod * a).astype(BF16)
    g1[...] += dot_tn(x, dpre_b)
    g2[...] += dot_tn(h, dm)
    bias_ref[...] += jnp.sum(dpre, axis=0, keepdims=True)
    local_ref[...] += dot(pick_cols(loc, inner_n), jnp.concatenate([m, da], axis=1))
    acc_r[...] += dot(pick_cols(rem, slots_n), jnp.concatenate([m, db], axis=1))

    @pl.when(step == pl.num_programs(0) - 1)
    def _():
        slot_ref[...] = acc_r[...].astype(BF16)
        n_in = g1.shape[0]
        grad_ref[:n_in, :] = g1[...].astype(BF16)
        for k in range(g2.shape[0] // width):
            grad_ref[n_in:, k * width : (k + 1) * width] = g2[k * width : (k + 1) * width, :].astype(BF16)


def final_kernel(rows_ref, ret_ref, local_ref, edges_ref, cot_ref, new_ref, grad_ref):
    tile, width = edges_ref.shape
    hot = pick_cols(rows_ref[...], tile, pl.program_id(0) * tile)
    total = local_ref[...] + dot(hot, ret_ref[...])
    new_ref[...] = (edges_ref[...].astype(F32) + total[:, :width]).astype(BF16)
    grad_ref[...] = (cot_ref[...].astype(F32) + total[:, width:]).astype(BF16)


def full(shape):
    return pl.BlockSpec(shape, lambda i: (0,) * len(shape))


def params():
    return pltpu.CompilerParams(dimension_semantics=("arbitrary",), vmem_limit_bytes=VMEM_LIMIT)


def tile_of(n, want):
    return want if n % want == 0 else n


def local(
    edges, cotangent, send_rows, send_count, trip_local, trip_remote, w_first, bias_first, w_second
):
    n_edges, width = edges.shape
    n_in, hid = w_first.shape
    ndev = lax.axis_size("phi") * lax.axis_size("eta")
    cap = send_rows.shape[2]
    slots = ndev * cap
    n_trip = trip_local.shape[0]
    live = jnp.arange(cap, dtype=jnp.int32)[None, :] < send_count[0][:, None]
    rows = jnp.where(live, send_rows[0], -1)

    st = tile_of(slots, 512)
    outgoing = pl.pallas_call(
        send_kernel,
        grid=(slots // st,),
        in_specs=[
            pl.BlockSpec((1, 1, st), lambda i: (i, 0, 0)),
            full((n_edges, width)),
            full((n_edges, width)),
        ],
        out_specs=pl.BlockSpec((st, 2 * width), lambda i: (i, 0)),
        out_shape=jax.ShapeDtypeStruct((slots, 2 * width), BF16),
        scratch_shapes=[pltpu.VMEM((n_edges, 2 * width), BF16)],
        compiler_params=params(),
        name="send_rows",
    )(rows.reshape(slots // st, 1, st), edges, cotangent)
    arrived = lax.all_to_all(outgoing, AXES, split_axis=0, concat_axis=0, tiled=True)

    tt = tile_of(n_trip, 1024)
    steps = n_trip // tt
    pack = n_in + hid * width // hid
    near_sum, slot_sum, grads, bias = pl.pallas_call(
        main_kernel,
        grid=(steps,),
        in_specs=[
            pl.BlockSpec((1, 1, tt), lambda i: (i, 0, 0)),
            pl.BlockSpec((1, 1, tt), lambda i: (i, 0, 0)),
            full((n_edges, width)),
            full((n_edges, width)),
            full((slots, 2 * width)),
            full((n_in, hid)),
            full((1, hid)),
            full((hid, width)),
        ],
        out_specs=[
            full((n_edges, 2 * width)),
            full((slots, 2 * width)),
            full((pack, hid)),
            full((1, hid)),
        ],
        out_shape=[
            jax.ShapeDtypeStruct((n_edges, 2 * width), F32),
            jax.ShapeDtypeStruct((slots, 2 * width), BF16),
            jax.ShapeDtypeStruct((pack, hid), BF16),
            jax.ShapeDtypeStruct((1, hid), F32),
        ],
        scratch_shapes=[
            pltpu.VMEM((n_edges, 2 * width), BF16),
            pltpu.VMEM((slots, 2 * width), F32),
            pltpu.VMEM((n_in, hid), F32),
            pltpu.VMEM((hid, width), F32),
        ],
        compiler_params=params(),
        name="triplets",
    )(
        trip_local.reshape(steps, 1, tt),
        trip_remote.reshape(steps, 1, tt),
        edges,
        cotangent,
        arrived,
        w_first,
        bias_first.reshape(1, hid),
        w_second,
    )

    share = pack // ndev
    payload = jnp.concatenate(
        [slot_sum.reshape(ndev, cap, 2 * width), grads.reshape(ndev, share, hid)], axis=1
    )
    back = lax.all_to_all(payload, AXES, split_axis=0, concat_axis=0, tiled=True)
    returned = back[:, :cap].reshape(slots, 2 * width)
    part = jnp.sum(back[:, cap:].astype(F32), axis=0)
    gathered = lax.all_gather(jnp.concatenate([part, bias], axis=0), AXES)
    packed = gathered[:, :share].reshape(pack, hid)
    grad_first = packed[:n_in]
    grad_second = jnp.concatenate(
        [packed[n_in:, k * width : (k + 1) * width] for k in range(hid // width)], axis=0
    )
    grad_bias = jnp.sum(gathered[:, share], axis=0)

    et = tile_of(n_edges, 512)
    row_block = lambda w: pl.BlockSpec((et, w), lambda i: (i, 0))
    new_edges, edge_grad = pl.pallas_call(
        final_kernel,
        grid=(n_edges // et,),
        in_specs=[
            full((1, slots)),
            full((slots, 2 * width)),
            row_block(2 * width),
            row_block(width),
            row_block(width),
        ],
        out_specs=[row_block(width), row_block(width)],
        out_shape=[jax.ShapeDtypeStruct((n_edges, width), BF16)] * 2,
        compiler_params=params(),
        name="add_up",
    )(rows.reshape(1, slots), returned, near_sum, edges, cotangent)
    return (new_edges, edge_grad, grad_first, grad_bias, grad_second)


def solution(mesh):
    spec = P(AXES, None)
    in_specs = (spec, spec, P(AXES, None, None), spec, P(AXES), P(AXES), P(), P(), P())
    out_specs = (spec, spec, P(), P(), P())
    return jax.shard_map(local, mesh=mesh, in_specs=in_specs, out_specs=out_specs, check_vma=False)
```

time: 521 us -> 184 us (0.35)
  other arithmetic: 217 us -> 6.03 us
  local copies, waits for them, and re-layouts: 128 us -> 3.54 us
  Pallas kernels: 0 us -> 56.9 us
  blocking collectives: 40.6 us -> 92.7 us
  waiting for transfers between devices: 72 us -> 21 us
  matrix products: 35.3 us -> 0 us
  between operations: 14.3 us -> 0.71 us
  starting transfers between devices: 13.3 us -> 2.62 us
    scatter-add x6 -> x0, other arithmetic: 192 us -> none  [the longest x1 45.7 us: local(): slot_grad = jax.ops.segment_sum(d_outer, trip_remote, ndev * slots_per)]
    gather x4 -> x0, local copies, waits for them, and re-layouts: 115 us -> none  [the longest x1 53.3 us: local(): outer_pair = arrived[trip_remote]]
    psum x1 -> x0, waiting for transfers between devices: 71.9 us -> none  [local(): lax.psum((grad_first, grad_bias, grad_second), ('phi', 'eta'))]
    all_gather x0 -> x1, blocking collectives: none -> 69 us  [local(): gathered = lax.all_gather(jnp.concatenate([part, bias], axis=0), AXES)]
    pallas_call x0 -> x3, Pallas kernels: none -> 56.9 us  [the longest x1 48.4 us: local(): pl.pallas_call(main_kernel, grid=(steps,), in_specs=[pl.BlockSpec((1, 1,...]
    psum x1 -> x0, blocking collectives: 40.6 us -> none  [local(): lax.psum((grad_first, grad_bias, grad_second), ('phi', 'eta'))]
    dot_general x6 -> x0, matrix products: 35.3 us -> none  [the longest x1 7.92 us: local(): jnp.dot(dmsg, w_second.T, preferred_element_type=jnp.float32)]
    all_to_all x0 -> x1, blocking collectives: none -> 23.7 us  [local(): lax.all_to_all(outgoing, AXES, split_axis=0, concat_axis=0, tiled=True)]
  transfers between devices with their start and end apart: 3 -> 1, of which waited for: 1 -> 1; matrix products, arithmetic and copies ran while one was open for 34% -> 0% of each run, Pallas kernels for 0% -> 0%
where the time goes in v1:
time: 184 us; the launch traced here: 183 us
  blocking collectives  92.7 us (50%)
  Pallas kernels  56.9 us (31%)
  waiting for transfers between devices  21 us (11%)
  other arithmetic  6.03 us (3%)
  local copies, waits for them, and re-layouts  3.54 us (2%)
  starting transfers between devices  2.62 us (1%)
    all_gather x1, blocking collectives, local(): gathered = lax.all_gather(jnp.concatenate([part, bias], axis=0), AXES)  69 us
    pallas_call x1, Pallas kernels, local(): pl.pallas_call(main_kernel, grid=(steps,), in_specs=[pl.BlockSpec((1, 1,...  48.4 us
    all_to_all x1, blocking collectives, local(): lax.all_to_all(outgoing, AXES, split_axis=0, concat_axis=0, tiled=True)  23.7 us
    all_to_all x1, waiting for transfers between devices, local(): lax.all_to_all(payload, AXES, split_axis=0, concat_axis=0, tiled=True)  21 us
    pallas_call x1, Pallas kernels, local(): pl.pallas_call(final_kernel, grid=(n_edges // et,), in_specs=[full((1, sl...  4.81 us
  transfers between devices with their start and end apart: 1, of which 1 were waited for; matrix products, arithmetic and copies ran while one was open for 0% of the time, Pallas kernels for 0%

profile of v1, /device:TPU:0, one launch (start us, length us, event | category | flops | bytes accessed | tf_op | source)
XLA Modules:
  0.0 183.4 jit_solution(1601474618526730467)
XLA Ops:
  0.6 0.5 broadcast.39
  1.1 1.3 reduce.4
  2.5 0.1 lt.54
  2.5 0.8 squeeze.7
  3.3 0.1 lt.52
  3.4 0.1 lt.55
  3.5 0.1 lt.56
  3.6 0.6 compare_select_fusion.rows_ref
  4.2 3.6 %send_rows.1 = bf16[1024,256]{1,0:T(8,128)(2,1)} custom-call(s32[2,1,512]{2,1,0:T(1,128)} %compare_select_fusion.rows_ref, bf16[2048,128]{1,0:T(8,128)(2,1)} %edges_ref.5, bf16[2048,128]{1,0:T(8,128)(2,1)} %cot_ref.5), custom_call_target="tpu_custom_call" | custom-call | tf_op jit(solution)/shard_map/send_rows/pallas_call | solution.py:138
  7.8 23.7 %all_to_all.16 = bf16[32,32,256]{2,1,0:T(8,128)(2,1)} all-to-all(bf16[32,32,256]{2,1,0:T(8,128)(2,1)} %bitcast.14), channel_id=1, replica_groups=mesh['phi'=4,'eta'=8] {'phi','eta'}, dimensions={0} | all-to-all | bytes 1048576 | tf_op jit(solution)/shard_map/all_to_all | solution.py:152
  31.5 48.4 %triplets.1 = (f32[2048,256]{1,0:T(8,128)}, bf16[1024,256]{1,0:T(8,128)(2,1)}, bf16[512,256]{1,0:T(8,128)(2,1)}, f32[1,256]{1,0:T(1,128)}) custom-call(s32[8,1,1024]{2,1,0:T(1,128)} %bitcast.20, s32[8,1,1024]{2,1,0:T(1,128)} %bitcast.21, bf16[2048,128]{1,0:T(8,128)(2,1)} %edges_ref.5, bf16[2048,128]{1,0:T(8,128)(2,1)} %cot_ref.5, ...), custom_call_target="tpu_custom_call" | custom-call | tf_op jit(solution)/shard_map/triplets/pallas_call | solution.py:157
  79.9 0.0 copy-start
  79.9 0.0 copy-start.2
  79.9 0.0 copy-start.1
  79.9 2.1 %pad_maximum_fusion = bf16[32,48,256]{2,1,0:T(8,128)(2,1)} fusion(bf16[32,16,256]{2,1,0:T(8,128)(2,1)} %bitcast.19, bf16[32,32,256]{2,1,0:T(8,128)(2,1)} %bitcast.17), kind=kLoop, calls=%fused_computation | loop fusion | flops 1572864 | bytes 1572864 | tf_op jit(solution)/shard_map/concatenate | solution.py:202
  82.0 2.6 %all-to-all-start.1 = ((bf16[32,48,256]{2,1,0:T(8,128)(2,1)}), bf16[32,48,256]{2,1,0:T(8,128)(2,1)S(1)}, u32[]{:S(2)}, u32[]{:S(2)}) async-start(bf16[32,48,256]{2,1,0:T(8,128)(2,1)} %pad_maximum_fusion), calls=%async_computation.1 | async-start | bytes 1572864 | tf_op jit(solution)/shard_map/all_to_all | solution.py:205
  84.7 0.0 copy-done
  84.7 0.1 squeeze.6
  84.8 0.0 copy-done.2
  84.8 0.1 iota_compare_fusion
  84.8 0.1 lt.50
  84.9 0.6 broadcast_select_fusion.rows_ref
  85.5 21.0 %all-to-all-done.1 = bf16[32,48,256]{2,1,0:T(8,128)(2,1)S(1)} async-done(((bf16[32,48,256]{2,1,0:T(8,128)(2,1)}), bf16[32,48,256]{2,1,0:T(8,128)(2,1)S(1)}, u32[]{:S(2)}, u32[]{:S(2)}) %all-to-all-start.1) | async-done | bytes 786464 | tf_op jit(solution)/shard_map/all_to_all | solution.py:205
  106.6 0.0 copy-done.1
  106.6 69.0 %all-gather.1 = f32[32,17,256]{2,1,0:T(8,128)S(1)} all-gather(f32[1,17,256]{2,1,0:T(8,128)S(1)} %maximum_bitcast_fusion), channel_id=2, replica_groups=mesh['phi'=4,'eta'=8] {'phi','eta'}, dimensions={0}, use_global_device_ids=true | all-gather | bytes 574464 | tf_op jit(solution)/shard_map/all_gather | solution.py:208
  175.6 0.6 slice_reduce_fusion
  176.2 0.8 slice.35
  177.0 0.1 slice.37
  177.1 0.7 pad_maximum_fusion.1
  177.7 0.9 slice.33
  178.6 4.8 %add_up.1 = (bf16[2048,128]{1,0:T(8,128)(2,1)}, bf16[2048,128]{1,0:T(8,128)(2,1)}) custom-call(s32[1,1024]{1,0:T(1,128)} %broadcast_select_fusion.rows_ref, bf16[1024,256]{1,0:T(8,128)(2,1)} %bitcast.15, f32[2048,256]{1,0:T(8,128)} %get-tuple-element.13.local_ref, bf16[2048,128]{1,0:T(8,128)(2,1)} %edges_ref.5, bf16[2048,128]{1,0:T(8,128)(2,1)} %cot_ref.5), custom_call_target="tpu_custom_call" | custom-call | tf_op jit(solution)/shard_map/add_up/pallas_call | solution.py:218
  (4 shorter events, 0.1 us)
Async XLA Ops:
  79.9 4.8 %copy-start = (s32[1,32,32]{2,1,0:T(8,128)S(1)}, s32[1,32,32]{2,1,0:T(8,128)}, u32[]{:S(2)}) copy-start(s32[1,32,32]{2,1,0:T(8,128)} %param.11) | copy-start | bytes 12292
  79.9 4.8 %copy-start.2 = (s32[1,32]{1,0:T(1,128)S(1)}, s32[1,32]{1,0:T(1,128)}, u32[]{:S(2)}) copy-start(s32[1,32]{1,0:T(1,128)} %param.12) | copy-start | bytes 388
  79.9 26.6 %copy-start.1 = (f32[1,256]{1,0:T(1,128)S(1)}, f32[1,256]{1,0:T(1,128)}, u32[]{:S(2)}) copy-start(f32[1,256]{1,0:T(1,128)} %get-tuple-element.16) | copy-start | bytes 3076
  82.0 24.5 %all-to-all-start.1 = ((bf16[32,48,256]{2,1,0:T(8,128)(2,1)}), bf16[32,48,256]{2,1,0:T(8,128)(2,1)S(1)}, u32[]{:S(2)}, u32[]{:S(2)}) async-start(bf16[32,48,256]{2,1,0:T(8,128)(2,1)} %pad_maximum_fusion), calls=%async_computation.1 | async-start | bytes 1572864 | tf_op jit(solution)/shard_map/all_to_all | solution.py:205

commit v2 on v1

v2 whole, which is shorter than its diff:
```python
import functools

import jax
import jax.numpy as jnp
from jax import lax
from jax.experimental import pallas as pl
from jax.experimental.pallas import tpu as pltpu
from jax.sharding import PartitionSpec as P

AXES = ("phi", "eta")
F32 = jnp.float32
BF16 = jnp.bfloat16
VMEM_LIMIT = 60 * 1024 * 1024


def dot(a, b):
    return jnp.dot(a, b, preferred_element_type=F32)


def dot_nt(a, b):
    return lax.dot_general(a, b, (((1,), (1,)), ((), ())), preferred_element_type=F32)


def dot_tn(a, b):
    return lax.dot_general(a, b, (((0,), (0,)), ((), ())), preferred_element_type=F32)


def pick_rows(idx, n):
    t = idx.shape[1]
    cols = jnp.broadcast_to(idx, (128, t)).T
    lane = lax.broadcasted_iota(jnp.int32, (t, 128), 1)
    parts = [jnp.where(cols - 128 * j == lane, 1.0, 0.0).astype(BF16) for j in range(n // 128)]
    return jnp.concatenate(parts, axis=1)


def pick_cols(idx, n, start=0):
    row = lax.broadcasted_iota(jnp.int32, (n, idx.shape[1]), 0)
    return jnp.where(row == idx - start, 1.0, 0.0).astype(BF16)


def send_kernel(rows_ref, edges_ref, cot_ref, out_ref, ec):
    width = edges_ref.shape[1]

    @pl.when(pl.program_id(0) == 0)
    def _():
        ec[:, :width] = edges_ref[...]
        ec[:, width:] = cot_ref[...]

    out_ref[...] = dot(pick_rows(rows_ref[0], ec.shape[0]), ec[...]).astype(BF16)


def near_kernel(loc_ref, edges_ref, cot_ref, out_ref, ec):
    width = edges_ref.shape[1]

    @pl.when(pl.program_id(0) == 0)
    def _():
        ec[:, :width] = edges_ref[...]
        ec[:, width:] = cot_ref[...]

    out_ref[...] = dot(pick_rows(loc_ref[0], ec.shape[0]), ec[...]).astype(BF16)


def main_kernel(
    fused, rem_ref, near_ref, arr_ref, w1_ref, b1_ref, w2_ref,
    mda_ref, slot_ref, grad_ref, bias_ref,
    acc_r, g1, g2,
):
    step = pl.program_id(0)
    width = w2_ref.shape[1]
    slots_n = arr_ref.shape[0]

    @pl.when(step == 0)
    def _():
        acc_r[...] = jnp.zeros_like(acc_r)
        g1[...] = jnp.zeros_like(g1)
        g2[...] = jnp.zeros_like(g2)
        bias_ref[...] = jnp.zeros_like(bias_ref)

    rem = rem_ref[0]
    far = dot(pick_rows(rem, slots_n), arr_ref[...])
    a_b = near_ref[:, :width]
    a = a_b.astype(F32)
    b = far[:, :width]
    dm = (near_ref[:, width:].astype(F32) + far[:, width:]).astype(BF16)
    x = jnp.concatenate([a_b, b.astype(BF16), (a * b).astype(BF16)], axis=1)
    pre = dot(x, w1_ref[...]) + b1_ref[...]
    sig = 0.5 * jnp.tanh(0.5 * pre) + 0.5
    h = (pre * sig).astype(BF16)
    m = dot(h, w2_ref[...]).astype(BF16)
    dpre = dot_nt(dm, w2_ref[...]) * (sig * (1.0 + pre * (1.0 - sig)))
    dpre_b = dpre.astype(BF16)
    dx = dot_nt(dpre_b, w1_ref[...])
    dprod = dx[:, 2 * width :]
    mda_ref[:, :width] = m
    mda_ref[:, width:] = (dx[:, :width] + dprod * b).astype(BF16)
    db = (dx[:, width : 2 * width] + dprod * a).astype(BF16)
    g1[...] += dot_tn(x, dpre_b)
    g2[...] += dot_tn(h, dm)
    bias_ref[...] += jnp.sum(dpre, axis=0, keepdims=True)
    acc_r[...] += dot(pick_cols(rem, slots_n), jnp.concatenate([m, db], axis=1))

    @pl.when(step == pl.num_programs(0) - 1)
    def _():
        second = jnp.concatenate(
            [g2[k * width : (k + 1) * width, :] for k in range(g2.shape[0] // width)], axis=1
        )
        if fused:
            ndev, both, wide = slot_ref.shape
            cap = slots_n // ndev
            share = both - cap
            slot_ref[:, :cap, :] = acc_r[...].astype(BF16).reshape(ndev, cap, wide)
            split = g1.shape[0] // share
            slot_ref[:split, cap:, :] = g1[...].astype(BF16).reshape(split, share, wide)
            slot_ref[split:, cap:, :] = second.astype(BF16).reshape(ndev - split, share, wide)
            grad_ref[...] = jnp.zeros_like(grad_ref)
        else:
            n_in = g1.shape[0]
            slot_ref[...] = acc_r[...].astype(BF16)
            grad_ref[:n_in, :] = g1[...].astype(BF16)
            grad_ref[n_in:, :] = second.astype(BF16)


def scatter_kernel(loc_ref, mda_ref, out_ref):
    @pl.when(pl.program_id(0) == 0)
    def _():
        out_ref[...] = jnp.zeros_like(out_ref)

    out_ref[...] += dot(pick_cols(loc_ref[0], out_ref.shape[0]), mda_ref[...])


def gather_kernel(
    n_phi, n_eta, back_ref, bias_ref, out_ref, outb_ref, buf, bufb, send_sem, recv_sem, send_b, recv_b
):
    phi = lax.axis_index("phi")
    eta = lax.axis_index("eta")
    me = phi * n_eta + eta
    pairs = n_phi // 2
    cap = back_ref.shape[1] - buf.shape[1]
    buf[me] = jnp.sum(back_ref[:, cap:, :].astype(F32), axis=0).astype(BF16)
    bufb[me] = bias_ref[...]
    row = [(phi, lax.rem(eta + k, n_eta)) for k in range(1, n_eta)]
    column = [(lax.rem(phi + 2 * k, n_phi), eta) for k in range(1, pairs)]
    mate = (phi + 1 - 2 * lax.rem(phi, 2), eta)

    barrier = pltpu.get_barrier_semaphore()
    peers = row + column + [mate]
    for peer in peers:
        pl.semaphore_signal(barrier, inc=1, device_id=peer, device_id_type=pl.DeviceIdType.MESH)
    pl.semaphore_wait(barrier, len(peers))

    slot = 0
    for stage in range(3):
        if stage == 0:
            moves = [(peer, me, 1) for peer in row]
        elif stage == 1:
            moves = [(peer, phi * n_eta, n_eta) for peer in column]
        else:
            own = lax.rem(phi, 2)
            moves = [(mate, (own + 2 * k) * n_eta, n_eta) for k in range(pairs)]
        copies = []
        for peer, start, count in moves:
            for data, sends, recvs in ((buf, send_sem, recv_sem), (bufb, send_b, recv_b)):
                part = data.at[pl.ds(start, count)]
                copies.append(
                    pltpu.make_async_remote_copy(
                        src_ref=part,
                        dst_ref=part,
                        send_sem=sends.at[slot],
                        recv_sem=recvs.at[slot],
                        device_id=peer,
                        device_id_type=pl.DeviceIdType.MESH,
                    )
                )
            slot += 1
        for copy in copies:
            copy.start()
        for copy in copies:
            copy.wait()
    out_ref[...] = buf[...]
    outb_ref[...] = bufb[...]


def final_kernel(
    rows_ref, back_ref, local_ref, edges_ref, cot_ref, pack_ref, bias_ref,
    new_ref, grad_ref, g1_ref, g2_ref, gb_ref,
):
    tile, width = edges_ref.shape
    ndev = back_ref.shape[0]
    slots = rows_ref.shape[1]
    hot = pick_cols(rows_ref[...], tile, pl.program_id(0) * tile)
    returned = back_ref[:, : slots // ndev, :].reshape(slots, 2 * width)
    total = local_ref[...] + dot(hot, returned)
    new_ref[...] = (edges_ref[...].astype(F32) + total[:, :width]).astype(BF16)
    grad_ref[...] = (cot_ref[...].astype(F32) + total[:, width:]).astype(BF16)

    @pl.when(pl.program_id(0) == 0)
    def _():
        n_in = g1_ref.shape[0]
        g1_ref[...] = pack_ref[:n_in, :].astype(F32)
        for k in range(g2_ref.shape[0] // width):
            g2_ref[k * width : (k + 1) * width, :] = pack_ref[n_in:, k * width : (k + 1) * width].astype(F32)
        gb_ref[...] = jnp.sum(bias_ref[...], axis=0)


def full(shape):
    return pl.BlockSpec(shape, lambda i: (0,) * len(shape))


def params():
    return pltpu.CompilerParams(dimension_semantics=("arbitrary",), vmem_limit_bytes=VMEM_LIMIT)


def tile_of(n, want):
    return want if n % want == 0 else n


def local(
    edges, cotangent, send_rows, send_count, trip_local, trip_remote, w_first, bias_first, w_second
):
    n_edges, width = edges.shape
    n_in, hid = w_first.shape
    ndev = lax.axis_size("phi") * lax.axis_size("eta")
    cap = send_rows.shape[2]
    slots = ndev * cap
    n_trip = trip_local.shape[0]
    live = jnp.arange(cap, dtype=jnp.int32)[None, :] < send_count[0][:, None]
    rows = jnp.where(live, send_rows[0], -1)

    st = tile_of(slots, 512)
    outgoing = pl.pallas_call(
        send_kernel,
        grid=(slots // st,),
        in_specs=[
            pl.BlockSpec((1, 1, st), lambda i: (i, 0, 0)),
            full((n_edges, width)),
            full((n_edges, width)),
        ],
        out_specs=pl.BlockSpec((st, 2 * width), lambda i: (i, 0)),
        out_shape=jax.ShapeDtypeStruct((slots, 2 * width), BF16),
        scratch_shapes=[pltpu.VMEM((n_edges, 2 * width), BF16)],
        compiler_params=params(),
        name="send_rows",
    )(rows.reshape(slots // st, 1, st), edges, cotangent)
    arrived = lax.all_to_all(outgoing, AXES, split_axis=0, concat_axis=0, tiled=True)

    tt = tile_of(n_trip, 1024)
    steps = n_trip // tt
    wide = 2 * width
    pack = n_in + width
    share = pack // ndev
    loc = trip_local.reshape(steps, 1, tt)
    rem = trip_remote.reshape(steps, 1, tt)
    idx_block = pl.BlockSpec((1, 1, tt), lambda i: (i, 0, 0))
    trip_block = pl.BlockSpec((tt, wide), lambda i: (i, 0))
    near = pl.pallas_call(
        near_kernel,
        grid=(steps,),
        in_specs=[idx_block, full((n_edges, width)), full((n_edges, width))],
        out_specs=trip_block,
        out_shape=jax.ShapeDtypeStruct((n_trip, wide), BF16),
        scratch_shapes=[pltpu.VMEM((n_edges, wide), BF16)],
        compiler_params=params(),
        cost_estimate=pl.CostEstimate(
            flops=2 * n_trip * n_edges * wide, bytes_accessed=2 * n_trip * wide, transcendentals=0
        ),
        name="near_rows",
    )(loc, edges, cotangent)

    fused = share % 16 == 0 and n_in % share == 0 and cap % 16 == 0
    if fused:
        slot_shape, grad_shape = (ndev, cap + share, wide), (8, hid)
    else:
        slot_shape, grad_shape = (slots, wide), (pack, hid)
    mda, payload, grads, bias = pl.pallas_call(
        functools.partial(main_kernel, fused),
        grid=(steps,),
        in_specs=[
            idx_block,
            trip_block,
            full((slots, wide)),
            full((n_in, hid)),
            full((1, hid)),
            full((hid, width)),
        ],
        out_specs=[trip_block, full(slot_shape), full(grad_shape), full((1, hid))],
        out_shape=[
            jax.ShapeDtypeStruct((n_trip, wide), BF16),
            jax.ShapeDtypeStruct(slot_shape, BF16),
            jax.ShapeDtypeStruct(grad_shape, BF16),
            jax.ShapeDtypeStruct((1, hid), F32),
        ],
        scratch_shapes=[
            pltpu.VMEM((slots, wide), F32),
            pltpu.VMEM((n_in, hid), F32),
            pltpu.VMEM((hid, width), F32),
        ],
        compiler_params=params(),
        cost_estimate=pl.CostEstimate(
            flops=12 * n_trip * n_in * hid, bytes_accessed=8 * n_trip * wide, transcendentals=0
        ),
        name="triplets",
    )(rem, near, arrived, w_first, bias_first.reshape(1, hid), w_second)
    if not fused:
        payload = jnp.concatenate(
            [payload.reshape(ndev, cap, wide), grads.reshape(ndev, share, hid)], axis=1
        )
    back = lax.all_to_all(payload, AXES, split_axis=0, concat_axis=0, tiled=True)

    near_sum = pl.pallas_call(
        scatter_kernel,
        grid=(steps,),
        in_specs=[idx_block, trip_block],
        out_specs=full((n_edges, wide)),
        out_shape=jax.ShapeDtypeStruct((n_edges, wide), F32),
        compiler_params=params(),
        cost_estimate=pl.CostEstimate(
            flops=2 * n_trip * n_edges * wide, bytes_accessed=2 * n_trip * wide, transcendentals=0
        ),
        name="near_sum",
    )(loc, mda)

    n_phi, n_eta = lax.axis_size("phi"), lax.axis_size("eta")
    moves = n_eta - 1 + n_phi // 2 - 1 + n_phi // 2
    sems = pltpu.SemaphoreType.DMA((moves,))
    packed, biases = pl.pallas_call(
        functools.partial(gather_kernel, n_phi, n_eta),
        in_specs=[pl.BlockSpec(memory_space=pltpu.VMEM)] * 2,
        out_specs=[pl.BlockSpec(memory_space=pltpu.VMEM)] * 2,
        out_shape=[
            jax.ShapeDtypeStruct((ndev, share, hid), BF16),
            jax.ShapeDtypeStruct((ndev, 1, hid), F32),
        ],
        scratch_shapes=[
            pltpu.VMEM((ndev, share, hid), BF16),
            pltpu.VMEM((ndev, 1, hid), F32),
            sems,
            sems,
            sems,
            sems,
        ],
        compiler_params=pltpu.CompilerParams(
            collective_id=0, has_side_effects=True, vmem_limit_bytes=VMEM_LIMIT
        ),
        name="gather_grads",
    )(back, bias)

    et = tile_of(n_edges, 512)
    row_block = lambda w: pl.BlockSpec((et, w), lambda i: (i, 0))
    new_edges, edge_grad, grad_first, grad_second, grad_bias = pl.pallas_call(
        final_kernel,
        grid=(n_edges // et,),
        in_specs=[
            full((1, slots)),
            full((ndev, cap + share, wide)),
            row_block(wide),
            row_block(width),
            row_block(width),
            full((pack, hid)),
            full((ndev, 1, hid)),
        ],
        out_specs=[
            row_block(width),
            row_block(width),
            full((n_in, hid)),
            full((hid, width)),
            full((1, hid)),
        ],
        out_shape=[
            jax.ShapeDtypeStruct((n_edges, width), BF16),
            jax.ShapeDtypeStruct((n_edges, width), BF16),
            jax.ShapeDtypeStruct((n_in, hid), F32),
            jax.ShapeDtypeStruct((hid, width), F32),
            jax.ShapeDtypeStruct((1, hid), F32),
        ],
        compiler_params=params(),
        name="add_up",
    )(rows.reshape(1, slots), back, near_sum, edges, cotangent, packed.reshape(pack, hid), biases)
    return (new_edges, edge_grad, grad_first, grad_bias.reshape(hid), grad_second)


def solution(mesh):
    spec = P(AXES, None)
    in_specs = (spec, spec, P(AXES, None, None), spec, P(AXES), P(AXES), P(), P(), P())
    out_specs = (spec, spec, P(), P(), P())
    return jax.shard_map(local, mesh=mesh, in_specs=in_specs, out_specs=out_specs, check_vma=False)
```

time: 184 us -> 110 us (0.60)
  blocking collectives: 92.7 us -> 0 us
  Pallas kernels: 56.9 us -> 80.8 us
  waiting for transfers between devices: 21 us -> 11.7 us
  starting transfers between devices: 2.62 us -> 9.97 us
  other arithmetic: 6.03 us -> 2.6 us
    all_gather x1 -> x0, blocking collectives: 69 us -> none  [local(): gathered = lax.all_gather(jnp.concatenate([part, bias], axis=0), AXES)]
    all_to_all x1 -> x0, blocking collectives: 23.7 us -> none  [local(): lax.all_to_all(outgoing, AXES, split_axis=0, concat_axis=0, tiled=True)]
    pallas_call x1 -> x4, Pallas kernels: 48.4 us -> 71.9 us  [the longest x1 33.8 us: local(): pl.pallas_call(functools.partial(main_kernel, fused), grid=(steps,), in_s...]
    all_to_all x1, waiting for transfers between devices: 21 us -> 8.28 us  [local(): lax.all_to_all(payload, AXES, split_axis=0, concat_axis=0, tiled=True)]
    all_to_all x0 -> x1, starting transfers between devices: none -> 7.32 us  [local(): lax.all_to_all(outgoing, AXES, split_axis=0, concat_axis=0, tiled=True)]
    all_to_all x0 -> x1, waiting for transfers between devices: none -> 3.44 us  [local(): lax.all_to_all(outgoing, AXES, split_axis=0, concat_axis=0, tiled=True)]
    concatenate x2 -> x0, other arithmetic: 2.77 us -> none  [the longest x1 2.1 us: local(): jnp.concatenate([slot_sum.reshape(ndev, cap, 2 * width), grads.reshape(nd...]
  transfers between devices with their start and end apart: 1 -> 2, of which waited for: 1 -> 2; matrix products, arithmetic and copies ran while one was open for 0% -> 1% of each run, Pallas kernels for 0% -> 23%
where the time goes in v2:
time: 110 us; the launch traced here: 109 us
  Pallas kernels  80.8 us (73%)
  waiting for transfers between devices  11.7 us (11%)
  starting transfers between devices  9.97 us (9%)
  local copies, waits for them, and re-layouts  3.49 us (3%)
  other arithmetic  2.6 us (2%)
    pallas_call x1, Pallas kernels, local(): pl.pallas_call(functools.partial(main_kernel, fused), grid=(steps,), in_s...  33.8 us
    pallas_call x1, Pallas kernels, local(): pl.pallas_call(near_kernel, grid=(steps,), in_specs=[idx_block, full((n_e...  12.8 us
    pallas_call x1, Pallas kernels, local(): pl.pallas_call(scatter_kernel, grid=(steps,), in_specs=[idx_block, trip_b...  12.7 us
    pallas_call x1, Pallas kernels, local(): pl.pallas_call(functools.partial(gather_kernel, n_phi, n_eta), in_specs=[...  12.7 us
    all_to_all x1, waiting for transfers between devices, local(): lax.all_to_all(payload, AXES, split_axis=0, concat_axis=0, tiled=True)  8.28 us
    all_to_all x1, starting transfers between devices, local(): lax.all_to_all(outgoing, AXES, split_axis=0, concat_axis=0, tiled=True)  7.32 us
    pallas_call x1, Pallas kernels, local(): pl.pallas_call(final_kernel, grid=(n_edges // et,), in_specs=[full((1, sl...  5.22 us
    pallas_call x1, Pallas kernels, local(): pl.pallas_call(send_kernel, grid=(slots // st,), in_specs=[pl.BlockSpec((...  3.63 us
  transfers between devices with their start and end apart: 2, of which 2 were waited for; matrix products, arithmetic and copies ran while one was open for 1% of the time, Pallas kernels for 23%

profile of v2, /device:TPU:0, one launch (start us, length us, event | category | flops | bytes accessed | tf_op | source)
XLA Modules:
  0.0 109.2 jit_solution(6350337948257537246)
XLA Ops:
  0.6 0.5 broadcast.39
  1.1 1.3 %reduce.3 = s32[32]{0:T(128)S(1)} reduce(s32[1,32]{1,0:T(1,128)} %param.12, s32[]{:T(128)} %broadcast.39), dimensions={0}, to_apply=%param.12.reduce_sub_computation.3 | reduce | bytes 260 | tf_op args[3]
  2.5 0.1 lt.54
  2.5 0.1 lt.55
  2.6 0.1 lt.56
  2.7 0.1 lt.52
  2.8 0.8 squeeze.6
  3.6 0.6 compare_select_fusion.rows_ref
  4.2 3.6 %send_rows.1 = bf16[1024,256]{1,0:T(8,128)(2,1)} custom-call(s32[2,1,512]{2,1,0:T(1,128)} %compare_select_fusion.rows_ref, bf16[2048,128]{1,0:T(8,128)(2,1)} %edges_ref.5, bf16[2048,128]{1,0:T(8,128)(2,1)} %cot_ref.5), custom_call_target="tpu_custom_call" | custom-call | tf_op jit(solution)/shard_map/send_rows/pallas_call | solution.py:230
  7.8 7.3 %all-to-all-start = ((bf16[32,32,256]{2,1,0:T(8,128)(2,1)}), bf16[32,32,256]{2,1,0:T(8,128)(2,1)S(1)}, u32[]{:S(2)}, u32[]{:S(2)}) async-start(bf16[32,32,256]{2,1,0:T(8,128)(2,1)} %bitcast.8), calls=%async_computation | async-start | bytes 1048576 | tf_op jit(solution)/shard_map/all_to_all | solution.py:244
  15.1 12.8 %near_rows.1.near_ref = bf16[8192,256]{1,0:T(8,128)(2,1)} custom-call(s32[8,1,1024]{2,1,0:T(1,128)} %bitcast.13, bf16[2048,128]{1,0:T(8,128)(2,1)} %edges_ref.5, bf16[2048,128]{1,0:T(8,128)(2,1)} %cot_ref.5), custom_call_target="tpu_custom_call" | custom-call | flops 8589934592 | bytes 4194304 | tf_op jit(solution)/shard_map/near_rows/pallas_call | solution.py:255
  27.9 3.4 %all-to-all-done = bf16[32,32,256]{2,1,0:T(8,128)(2,1)S(1)} async-done(((bf16[32,32,256]{2,1,0:T(8,128)(2,1)}), bf16[32,32,256]{2,1,0:T(8,128)(2,1)S(1)}, u32[]{:S(2)}, u32[]{:S(2)}) %all-to-all-start) | async-done | bytes 524320 | tf_op jit(solution)/shard_map/all_to_all | solution.py:244
  31.4 0.0 copy-start.1
  31.4 0.8 copy-done.1
  32.2 0.0 copy-start.2
  32.2 0.0 copy-start.3
  32.2 33.8 %triplets.1 = (bf16[8192,256]{1,0:T(8,128)(2,1)}, bf16[32,48,256]{2,1,0:T(8,128)(2,1)}, bf16[8,256]{1,0:T(8,128)(2,1)}, f32[1,256]{1,0:T(1,128)}) custom-call(s32[8,1,1024]{2,1,0:T(1,128)} %bitcast.12, bf16[8192,256]{1,0:T(8,128)(2,1)} %near_rows.1.near_ref, bf16[1024,256]{1,0:T(8,128)(2,1)} %bitcast.9, bf16[384,256]{1,0:T(8,128)(2,1)} %w1_ref.1, ...), custom_call_target="tpu_custom_call" | custom-call | flops 9663676416 | bytes 16777216 | tf_op jit(solution)/shard_map/triplets/pallas_call | solution.py:274
  66.0 2.6 %all-to-all-start.1 = ((bf16[32,48,256]{2,1,0:T(8,128)(2,1)}), bf16[32,48,256]{2,1,0:T(8,128)(2,1)S(1)}, u32[]{:S(2)}, u32[]{:S(2)}) async-start(bf16[32,48,256]{2,1,0:T(8,128)(2,1)} %get-tuple-element.15), calls=%async_computation.1 | async-start | bytes 1572864 | tf_op jit(solution)/shard_map/all_to_all | solution.py:307
  68.6 0.0 copy-done.2
  68.6 0.1 squeeze.5
  68.7 0.0 copy-done.3
  68.7 0.1 iota_compare_fusion
  68.8 0.1 lt.50
  68.9 0.6 broadcast_select_fusion.rows_ref
  69.5 12.7 %near_sum.1.local_ref = f32[2048,256]{1,0:T(8,128)} custom-call(s32[8,1,1024]{2,1,0:T(1,128)} %bitcast.14, bf16[8192,256]{1,0:T(8,128)(2,1)} %get-tuple-element.16.mda_ref), custom_call_target="tpu_custom_call" | custom-call | flops 8589934592 | bytes 4194304 | tf_op jit(solution)/shard_map/near_sum/pallas_call | solution.py:309
  82.2 8.3 %all-to-all-done.1.back_ref = bf16[32,48,256]{2,1,0:T(8,128)(2,1)S(1)} async-done(((bf16[32,48,256]{2,1,0:T(8,128)(2,1)}), bf16[32,48,256]{2,1,0:T(8,128)(2,1)S(1)}, u32[]{:S(2)}, u32[]{:S(2)}) %all-to-all-start.1) | async-done | bytes 786464 | tf_op jit(solution)/shard_map/all_to_all | solution.py:307
  90.5 0.0 copy-start
  90.5 0.9 copy-done
  91.4 12.7 %gather_grads.1 = (bf16[32,16,256]{2,1,0:T(8,128)(2,1)}, f32[32,1,256]{2,1,0:T(1,128)}) custom-call(bf16[32,48,256]{2,1,0:T(8,128)(2,1)} %copy-done, f32[1,256]{1,0:T(1,128)} %get-tuple-element.17.bias_ref), custom_call_target="tpu_custom_call" | custom-call | tf_op jit(solution)/shard_map/gather_grads/pallas_call | solution.py:325
  104.0 5.2 %add_up.1 = (bf16[2048,128]{1,0:T(8,128)(2,1)}, bf16[2048,128]{1,0:T(8,128)(2,1)}, f32[384,256]{1,0:T(8,128)}, f32[256,128]{1,0:T(8,128)}, f32[1,256]{1,0:T(1,128)}) custom-call(s32[1,1024]{1,0:T(1,128)} %broadcast_select_fusion.rows_ref, bf16[32,48,256]{2,1,0:T(8,128)(2,1)} %copy-done, f32[2048,256]{1,0:T(8,128)} %near_sum.1.local_ref, ...), custom_call_target="tpu_custom_call" | custom-call | tf_op jit(solution)/shard_map/add_up/pallas_call | solution.py:349
  (1 shorter events, 0.0 us)
Async XLA Ops:
  7.8 23.6 %all-to-all-start = ((bf16[32,32,256]{2,1,0:T(8,128)(2,1)}), bf16[32,32,256]{2,1,0:T(8,128)(2,1)S(1)}, u32[]{:S(2)}, u32[]{:S(2)}) async-start(bf16[32,32,256]{2,1,0:T(8,128)(2,1)} %bitcast.8), calls=%async_computation | async-start | bytes 1048576 | tf_op jit(solution)/shard_map/all_to_all | solution.py:244
  31.4 0.8 copy-start.1
  32.2 36.5 %copy-start.2 = (s32[1,32,32]{2,1,0:T(8,128)S(1)}, s32[1,32,32]{2,1,0:T(8,128)}, u32[]{:S(2)}) copy-start(s32[1,32,32]{2,1,0:T(8,128)} %param.11) | copy-start | bytes 12292
  32.2 36.5 %copy-start.3 = (s32[1,32]{1,0:T(1,128)S(1)}, s32[1,32]{1,0:T(1,128)}, u32[]{:S(2)}) copy-start(s32[1,32]{1,0:T(1,128)} %param.12) | copy-start | bytes 388
  66.0 24.5 %all-to-all-start.1 = ((bf16[32,48,256]{2,1,0:T(8,128)(2,1)}), bf16[32,48,256]{2,1,0:T(8,128)(2,1)S(1)}, u32[]{:S(2)}, u32[]{:S(2)}) async-start(bf16[32,48,256]{2,1,0:T(8,128)(2,1)} %get-tuple-element.15), calls=%async_computation.1 | async-start | bytes 1572864 | tf_op jit(solution)/shard_map/all_to_all | solution.py:307
  90.5 0.9 copy-start

commit v3 on v2

--- a/solution.py
+++ b/solution.py
@@ -38,26 +38,83 @@
     return jnp.where(row == idx - start, 1.0, 0.0).astype(BF16)
 
 
-def send_kernel(rows_ref, edges_ref, cot_ref, out_ref, ec):
+MESH = pl.DeviceIdType.MESH
+
+
+def place(n_phi, n_eta):
+    phi = lax.axis_index("phi")
+    eta = lax.axis_index("eta")
+    return phi, eta, phi * n_eta + eta, n_phi * n_eta
+
+
+def greet_all(n_eta, me, ndev):
+    barrier = pltpu.get_barrier_semaphore()
+
+    def greet(k, carry):
+        peer = lax.rem(me + k, ndev)
+        pl.semaphore_signal(
+            barrier, inc=1, device_id=(peer // n_eta, lax.rem(peer, n_eta)), device_id_type=MESH
+        )
+        return carry
+
+    lax.fori_loop(1, ndev, greet, 0)
+    return barrier
+
+
+def exchange(n_eta, me, ndev, k, src, dst, send_sem, recv_sem):
+    peer = lax.rem(me + k, ndev)
+    return pltpu.make_async_remote_copy(
+        src_ref=src(peer),
+        dst_ref=dst(me),
+        send_sem=send_sem.at[k],
+        recv_sem=recv_sem.at[k],
+        device_id=(peer // n_eta, lax.rem(peer, n_eta)),
+        device_id_type=MESH,
+    )
+
+
+def near_kernel(
+    n_phi, n_eta, loc_ref, rows_ref, edges_ref, cot_ref, near_ref, arr_ref,
+    ec, outbox, inbox, send_sem, recv_sem,
+):
+    step = pl.program_id(0)
     width = edges_ref.shape[1]
-
-    @pl.when(pl.program_id(0) == 0)
-    def _():
+    phi, eta, me, ndev = place(n_phi, n_eta)
+    cap = outbox.shape[1]
+    copy_of = lambda k: exchange(
+        n_eta, me, ndev, k, lambda d: outbox.at[d], lambda d: inbox.at[d], send_sem, recv_sem
+    )
+
+    @pl.when(step == 0)
+    def _():
+        barrier = greet_all(n_eta, me, ndev)
         ec[:, :width] = edges_ref[...]
         ec[:, width:] = cot_ref[...]
-
-    out_ref[...] = dot(pick_rows(rows_ref[0], ec.shape[0]), ec[...]).astype(BF16)
-
-
-def near_kernel(loc_ref, edges_ref, cot_ref, out_ref, ec):
-    width = edges_ref.shape[1]
-
-    @pl.when(pl.program_id(0) == 0)
-    def _():
-        ec[:, :width] = edges_ref[...]
-        ec[:, width:] = cot_ref[...]
-
-    out_ref[...] = dot(pick_rows(loc_ref[0], ec.shape[0]), ec[...]).astype(BF16)
+        slots = ndev * cap
+        part = slots if slots < 1024 else 1024
+        for p in range(slots // part):
+            rows = rows_ref[:, p * part : (p + 1) * part]
+            picked = dot(pick_rows(rows, ec.shape[0]), ec[...]).astype(BF16)
+            outbox[p * part // cap : (p + 1) * part // cap] = picked.reshape(part // cap, cap, 2 * width)
+        inbox[me] = outbox[me]
+        pl.semaphore_wait(barrier, ndev - 1)
+
+        def send(k, carry):
+            copy_of(k).start()
+            return carry
+
+        lax.fori_loop(1, ndev, send, 0)
+
+    near_ref[...] = dot(pick_rows(loc_ref[0], ec.shape[0]), ec[...]).astype(BF16)
+
+    @pl.when(step == pl.num_programs(0) - 1)
+    def _():
+        def settle(k, carry):
+            copy_of(k).wait()
+            return carry
+
+        lax.fori_loop(1, ndev, settle, 0)
+        arr_ref[...] = inbox[...]
 
 
 def main_kernel(
@@ -120,46 +177,53 @@
             grad_ref[n_in:, :] = second.astype(BF16)
 
 
-def scatter_kernel(loc_ref, mda_ref, out_ref):
-    @pl.when(pl.program_id(0) == 0)
-    def _():
-        out_ref[...] = jnp.zeros_like(out_ref)
-
-    out_ref[...] += dot(pick_cols(loc_ref[0], out_ref.shape[0]), mda_ref[...])
-
-
-def gather_kernel(
-    n_phi, n_eta, back_ref, bias_ref, out_ref, outb_ref, buf, bufb, send_sem, recv_sem, send_b, recv_b
+def scatter_kernel(
+    n_phi, n_eta, loc_ref, mda_ref, pay_ref, bias_ref,
+    sum_ref, back_ref, out_ref, outb_ref,
+    shares, inbox, buf, bufb,
+    send_g, recv_g, send_s, recv_s, send_a, recv_a, send_b, recv_b,
 ):
-    phi = lax.axis_index("phi")
-    eta = lax.axis_index("eta")
-    me = phi * n_eta + eta
+    step = pl.program_id(0)
+    last = pl.num_programs(0) - 1
+    phi, eta, me, ndev = place(n_phi, n_eta)
+    cap = inbox.shape[1]
+    share = buf.shape[1]
     pairs = n_phi // 2
-    cap = back_ref.shape[1] - buf.shape[1]
-    buf[me] = jnp.sum(back_ref[:, cap:, :].astype(F32), axis=0).astype(BF16)
-    bufb[me] = bias_ref[...]
     row = [(phi, lax.rem(eta + k, n_eta)) for k in range(1, n_eta)]
     column = [(lax.rem(phi + 2 * k, n_phi), eta) for k in range(1, pairs)]
     mate = (phi + 1 - 2 * lax.rem(phi, 2), eta)
-
-    barrier = pltpu.get_barrier_semaphore()
-    peers = row + column + [mate]
-    for peer in peers:
-        pl.semaphore_signal(barrier, inc=1, device_id=peer, device_id_type=pl.DeviceIdType.MESH)
-    pl.semaphore_wait(barrier, len(peers))
-
-    slot = 0
-    for stage in range(3):
-        if stage == 0:
-            moves = [(peer, me, 1) for peer in row]
-        elif stage == 1:
-            moves = [(peer, phi * n_eta, n_eta) for peer in column]
-        else:
-            own = lax.rem(phi, 2)
-            moves = [(mate, (own + 2 * k) * n_eta, n_eta) for k in range(pairs)]
+    own = lax.rem(phi, 2)
+    stages = [
+        [(peer, me, 1) for peer in row],
+        [(peer, phi * n_eta, n_eta) for peer in column],
+        [(mate, (own + 2 * k) * n_eta, n_eta) for k in range(pairs)],
+    ]
+    bases = [0, len(row), len(row) + len(column)]
+
+    def grad_copy(k):
+        return exchange(
+            n_eta, me, ndev, k,
+            lambda d: pay_ref.at[d, pl.ds(cap, share)], lambda d: shares.at[d], send_g, recv_g,
+        )
+
+    def slot_copy(k):
+        return exchange(
+            n_eta, me, ndev, k,
+            lambda d: pay_ref.at[d, pl.ds(0, cap)], lambda d: inbox.at[d], send_s, recv_s,
+        )
+
+    def each(first, end, act):
+        def body(k, carry):
+            act(k)
+            return carry
+
+        lax.fori_loop(first, end, body, 0)
+
+    def stage_copies(stage):
         copies = []
-        for peer, start, count in moves:
-            for data, sends, recvs in ((buf, send_sem, recv_sem), (bufb, send_b, recv_b)):
+        for n, (peer, start, count) in enumerate(stages[stage]):
+            slot = bases[stage] + n
+            for data, sends, recvs in ((buf, send_a, recv_a), (bufb, send_b, recv_b)):
                 part = data.at[pl.ds(start, count)]
                 copies.append(
                     pltpu.make_async_remote_copy(
@@ -168,16 +232,59 @@
                         send_sem=sends.at[slot],
                         recv_sem=recvs.at[slot],
                         device_id=peer,
-                        device_id_type=pl.DeviceIdType.MESH,
+                        device_id_type=MESH,
                     )
                 )
-            slot += 1
-        for copy in copies:
+        return copies
+
+    def begin(stage):
+        for copy in stage_copies(stage):
             copy.start()
-        for copy in copies:
+
+    def finish(stage):
+        for copy in stage_copies(stage):
             copy.wait()
-    out_ref[...] = buf[...]
-    outb_ref[...] = bufb[...]
+
+    cut1, cut2 = 1 + (ndev - 1) // 3, 1 + 2 * (ndev - 1) // 3
+
+    @pl.when(step == 0)
+    def _():
+        barrier = greet_all(n_eta, me, ndev)
+        sum_ref[...] = jnp.zeros_like(sum_ref)
+        bufb[me] = bias_ref[...]
+        shares[me] = pay_ref[me, cap:, :]
+        inbox[me] = pay_ref[me, :cap, :]
+        pl.semaphore_wait(barrier, ndev - 1)
+        each(1, ndev, lambda k: grad_copy(k).start())
+        each(1, cut1, lambda k: slot_copy(k).start())
+
+    @pl.when(step == last // 2)
+    def _():
+        each(1, ndev, lambda k: grad_copy(k).wait())
+        buf[me] = jnp.sum(shares[...].astype(F32), axis=0).astype(BF16)
+
+    sum_ref[...] += dot(pick_cols(loc_ref[0], sum_ref.shape[0]), mda_ref[...])
+
+    @pl.when(step == last // 2)
+    def _():
+        begin(0)
+        each(cut1, cut2, lambda k: slot_copy(k).start())
+
+    @pl.when(step == last * 3 // 4)
+    def _():
+        finish(0)
+        begin(1)
+        each(cut2, ndev, lambda k: slot_copy(k).start())
+
+    @pl.when(step == last)
+    def _():
+        finish(1)
+        begin(2)
+        each(1, ndev, lambda k: slot_copy(k).wait())
+        back_ref[...] = inbox[...]
+        finish(2)
+        out_ref[...] = buf[...]
+        outb_ref[...] = bufb[...]
 
 
 def final_kernel(
@@ -188,7 +295,7 @@
     ndev = back_ref.shape[0]
     slots = rows_ref.shape[1]
     hot = pick_cols(rows_ref[...], tile, pl.program_id(0) * tile)
-    returned = back_ref[:, : slots // ndev, :].reshape(slots, 2 * width)
+    returned = back_ref[...].reshape(slots, 2 * width)
     total = local_ref[...] + dot(hot, returned)
     new_ref[...] = (edges_ref[...].astype(F32) + total[:, :width]).astype(BF16)
     grad_ref[...] = (cot_ref[...].astype(F32) + total[:, width:]).astype(BF16)
@@ -226,23 +333,6 @@
     live = jnp.arange(cap, dtype=jnp.int32)[None, :] < send_count[0][:, None]
     rows = jnp.where(live, send_rows[0], -1)
 
-    st = tile_of(slots, 512)
-    outgoing = pl.pallas_call(
-        send_kernel,
-        grid=(slots // st,),
-        in_specs=[
-            pl.BlockSpec((1, 1, st), lambda i: (i, 0, 0)),
-            full((n_edges, width)),
-            full((n_edges, width)),
-        ],
-        out_specs=pl.BlockSpec((st, 2 * width), lambda i: (i, 0)),
-        out_shape=jax.ShapeDtypeStruct((slots, 2 * width), BF16),
-        scratch_shapes=[pltpu.VMEM((n_edges, 2 * width), BF16)],
-        compiler_params=params(),
-        name="send_rows",
-    )(rows.reshape(slots // st, 1, st), edges, cotangent)
-    arrived = lax.all_to_all(outgoing, AXES, split_axis=0, concat_axis=0, tiled=True)
-
     tt = tile_of(n_trip, 1024)
     steps = n_trip // tt
     wide = 2 * width
@@ -252,19 +342,30 @@
     rem = trip_remote.reshape(steps, 1, tt)
     idx_block = pl.BlockSpec((1, 1, tt), lambda i: (i, 0, 0))
     trip_block = pl.BlockSpec((tt, wide), lambda i: (i, 0))
-    near = pl.pallas_call(
-        near_kernel,
+    n_phi, n_eta = lax.axis_size("phi"), lax.axis_size("eta")
+    flat = rows.reshape(1, slots)
+    remote = lambda n: pltpu.CompilerParams(
+        dimension_semantics=("arbitrary",),
+        collective_id=n,
+        has_side_effects=True,
+        vmem_limit_bytes=VMEM_LIMIT,
+    )
+    box = pltpu.VMEM((ndev, cap, wide), BF16)
+    each_dev = pltpu.SemaphoreType.DMA((ndev,))
+    near, arrived = pl.pallas_call(
+        functools.partial(near_kernel, n_phi, n_eta),
         grid=(steps,),
-        in_specs=[idx_block, full((n_edges, width)), full((n_edges, width))],
-        out_specs=trip_block,
-        out_shape=jax.ShapeDtypeStruct((n_trip, wide), BF16),
-        scratch_shapes=[pltpu.VMEM((n_edges, wide), BF16)],
-        compiler_params=params(),
-        cost_estimate=pl.CostEstimate(
-            flops=2 * n_trip * n_edges * wide, bytes_accessed=2 * n_trip * wide, transcendentals=0
-        ),
+        in_specs=[idx_block, full((1, slots)), full((n_edges, width)), full((n_edges, width))],
+        out_specs=[trip_block, full((ndev, cap, wide))],
+        out_shape=[
+            jax.ShapeDtypeStruct((n_trip, wide), BF16),
+            jax.ShapeDtypeStruct((ndev, cap, wide), BF16),
+        ],
+        scratch_shapes=[pltpu.VMEM((n_edges, wide), BF16), box, box, each_dev, each_dev],
+        compiler_params=remote(0),
         name="near_rows",
-    )(loc, edges, cotangent)
+    )(loc, flat, edges, cotangent)
+    arrived = arrived.reshape(slots, wide)
 
     fused = share % 16 == 0 and n_in % share == 0 and cap % 16 == 0
     if fused:
@@ -304,45 +405,35 @@
         payload = jnp.concatenate(
             [payload.reshape(ndev, cap, wide), grads.reshape(ndev, share, hid)], axis=1
         )
-    back = lax.all_to_all(payload, AXES, split_axis=0, concat_axis=0, tiled=True)
-
-    near_sum = pl.pallas_call(
-        scatter_kernel,
-        grid=(steps,),
-        in_specs=[idx_block, trip_block],
-        out_specs=full((n_edges, wide)),
-        out_shape=jax.ShapeDtypeStruct((n_edges, wide), F32),
-        compiler_params=params(),
-        cost_estimate=pl.CostEstimate(
-            flops=2 * n_trip * n_edges * wide, bytes_accessed=2 * n_trip * wide, transcendentals=0
-        ),
-        name="near_sum",
-    )(loc, mda)
-
-    n_phi, n_eta = lax.axis_size("phi"), lax.axis_size("eta")
     moves = n_eta - 1 + n_phi // 2 - 1 + n_phi // 2
     sems = pltpu.SemaphoreType.DMA((moves,))
-    packed, biases = pl.pallas_call(
-        functools.partial(gather_kernel, n_phi, n_eta),
-        in_specs=[pl.BlockSpec(memory_space=pltpu.VMEM)] * 2,
-        out_specs=[pl.BlockSpec(memory_space=pltpu.VMEM)] * 2,
+    near_sum, back, packed, biases = pl.pallas_call(
+        functools.partial(scatter_kernel, n_phi, n_eta),
+        grid=(steps,),
+        in_specs=[idx_block, trip_block, full((ndev, cap + share, wide)), full((1, hid))],
+        out_specs=[
+            full((n_edges, wide)),
+            full((ndev, cap, wide)),
+            full((ndev, share, hid)),
+            full((ndev, 1, hid)),
+        ],
         out_shape=[
+            jax.ShapeDtypeStruct((n_edges, wide), F32),
+            jax.ShapeDtypeStruct((ndev, cap, wide), BF16),
             jax.ShapeDtypeStruct((ndev, share, hid), BF16),
             jax.ShapeDtypeStruct((ndev, 1, hid), F32),
         ],
         scratch_shapes=[
             pltpu.VMEM((ndev, share, hid), BF16),
+            box,
+            pltpu.VMEM((ndev, share, hid), BF16),
             pltpu.VMEM((ndev, 1, hid), F32),
-            sems,
-            sems,
-            sems,
-            sems,
-        ],
-        compiler_params=pltpu.CompilerParams(
-            collective_id=0, has_side_effects=True, vmem_limit_bytes=VMEM_LIMIT
-        ),
-        name="gather_grads",
-    )(back, bias)
+        ]
+        + [each_dev] * 4
+        + [sems] * 4,
+        compiler_params=remote(1),
+        name="near_sum",
+    )(loc, mda, payload, bias)
 
     et = tile_of(n_edges, 512)
     row_block = lambda w: pl.BlockSpec((et, w), lambda i: (i, 0))
@@ -351,7 +442,7 @@
         grid=(n_edges // et,),
         in_specs=[
             full((1, slots)),
-            full((ndev, cap + share, wide)),
+            full((ndev, cap, wide)),
             row_block(wide),
             row_block(width),
             row_block(width),
@@ -374,7 +465,7 @@
         ],
         compiler_params=params(),
         name="add_up",
-    )(rows.reshape(1, slots), back, near_sum, edges, cotangent, packed.reshape(pack, hid), biases)
+    )(flat, back, near_sum, edges, cotangent, packed.reshape(pack, hid), biases)
     return (new_edges, edge_grad, grad_first, grad_bias.reshape(hid), grad_second)
 
 

time: 110 us -> 93.3 us (0.85)
  waiting for transfers between devices: 11.7 us -> 0 us
  starting transfers between devices: 9.97 us -> 0 us
  Pallas kernels: 80.8 us -> 90.1 us
  local copies, waits for them, and re-layouts: 3.49 us -> 0.89 us
  other arithmetic: 2.6 us -> 1.33 us
    all_to_all x2 -> x0, waiting for transfers between devices: 11.7 us -> none  [the longest x1 8.28 us: local(): lax.all_to_all(payload, AXES, split_axis=0, concat_axis=0, tiled=True)]
    all_to_all x2 -> x0, starting transfers between devices: 9.97 us -> none  [the longest x1 7.32 us: local(): lax.all_to_all(outgoing, AXES, split_axis=0, concat_axis=0, tiled=True)]
    pallas_call x4 -> x2, Pallas kernels: 41.8 us -> 51.2 us  [the longest x1 29.4 us: local(): pl.pallas_call(functools.partial(scatter_kernel, n_phi, n_eta), grid=(ste...]
    unnamed x9 -> x0, local copies, waits for them, and re-layouts: 2.2 us -> none
    unnamed x1 -> x0, other arithmetic: 1.32 us -> none
  transfers between devices with their start and end apart: 2 -> 0, of which waited for: 2 -> 0; matrix products, arithmetic and copies ran while one was open for 1% -> 0% of each run, Pallas kernels for 23% -> 0%
where the time goes in v3:
time: 93.3 us; the launch traced here: 93 us
  Pallas kernels  90.1 us (97%)
  other arithmetic  1.33 us (1%)
    pallas_call x1, Pallas kernels, local(): pl.pallas_call(functools.partial(main_kernel, fused), grid=(steps,), in_s...  33.8 us
    pallas_call x1, Pallas kernels, local(): pl.pallas_call(functools.partial(scatter_kernel, n_phi, n_eta), grid=(ste...  29.4 us
    pallas_call x1, Pallas kernels, local(): pl.pallas_call(functools.partial(near_kernel, n_phi, n_eta), grid=(steps,...  21.7 us
    pallas_call x1, Pallas kernels, local(): pl.pallas_call(final_kernel, grid=(n_edges // et,), in_specs=[full((1, sl...  5.14 us

profile of v3, /device:TPU:0, one launch (start us, length us, event | category | flops | bytes accessed | tf_op | source)
XLA Modules:
  0.0 93.0 jit_solution(3175278175907385698)
XLA Ops:
  0.6 0.8 squeeze.3
  1.4 0.7 iota_compare_fusion
  2.2 0.1 lt.29
  2.2 0.6 broadcast_select_fusion.rows_ref
  2.8 21.7 %near_rows.1 = (bf16[8192,256]{1,0:T(8,128)(2,1)}, bf16[32,32,256]{2,1,0:T(8,128)(2,1)}) custom-call(s32[8,1,1024]{2,1,0:T(1,128)} %bitcast.8, s32[1,1024]{1,0:T(1,128)} %broadcast_select_fusion.rows_ref, bf16[2048,128]{1,0:T(8,128)(2,1)} %edges_ref.3, bf16[2048,128]{1,0:T(8,128)(2,1)} %cot_ref.3), custom_call_target="tpu_custom_call" | custom-call | tf_op jit(solution)/shard_map/near_rows/pallas_call | solution.py:355
  24.6 33.8 %triplets.1 = (bf16[8192,256]{1,0:T(8,128)(2,1)}, bf16[32,48,256]{2,1,0:T(8,128)(2,1)}, bf16[8,256]{1,0:T(8,128)(2,1)}, f32[1,256]{1,0:T(1,128)}) custom-call(s32[8,1,1024]{2,1,0:T(1,128)} %bitcast.12, bf16[8192,256]{1,0:T(8,128)(2,1)} %get-tuple-element.19.near_ref, bf16[1024,256]{1,0:T(8,128)(2,1)} %bitcast.11, bf16[384,256]{1,0:T(8,128)(2,1)} %w1_ref.1, ...), custom_call_target="tpu_custom_call" | custom-call | flops 9663676416 | bytes 16777216 | tf_op jit(solution)/shard_map/triplets/pallas_call | solution.py:375
  58.4 29.4 %near_sum.1 = (f32[2048,256]{1,0:T(8,128)}, bf16[32,32,256]{2,1,0:T(8,128)(2,1)}, bf16[32,16,256]{2,1,0:T(8,128)(2,1)}, f32[32,1,256]{2,1,0:T(1,128)}) custom-call(s32[8,1,1024]{2,1,0:T(1,128)} %bitcast.9, bf16[8192,256]{1,0:T(8,128)(2,1)} %get-tuple-element.21.mda_ref, bf16[32,48,256]{2,1,0:T(8,128)(2,1)} %get-tuple-element.22.pay_ref, ...), custom_call_target="tpu_custom_call" | custom-call | tf_op jit(solution)/shard_map/near_sum/pallas_call | solution.py:410
  87.8 5.1 %add_up.1 = (bf16[2048,128]{1,0:T(8,128)(2,1)}, bf16[2048,128]{1,0:T(8,128)(2,1)}, f32[384,256]{1,0:T(8,128)}, f32[256,128]{1,0:T(8,128)}, f32[1,256]{1,0:T(1,128)}) custom-call(s32[1,1024]{1,0:T(1,128)} %broadcast_select_fusion.rows_ref, bf16[32,32,256]{2,1,0:T(8,128)(2,1)} %get-tuple-element.24.back_ref, f32[2048,256]{1,0:T(8,128)} %get-tuple-element.25.local_ref, ...), custom_call_target="tpu_custom_call" | custom-call | tf_op jit(solution)/shard_map/add_up/pallas_call | solution.py:440

commit v4 on v3

--- a/solution.py
+++ b/solution.py
@@ -10,6 +10,7 @@
 AXES = ("phi", "eta")
 F32 = jnp.float32
 BF16 = jnp.bfloat16
+TM = 512
 VMEM_LIMIT = 60 * 1024 * 1024
 
 
@@ -339,7 +340,8 @@
     pack = n_in + width
     share = pack // ndev
     loc = trip_local.reshape(steps, 1, tt)
-    rem = trip_remote.reshape(steps, 1, tt)
+    tm = tile_of(n_trip, TM)
+    rem = trip_remote.reshape(n_trip // tm, 1, tm)
     idx_block = pl.BlockSpec((1, 1, tt), lambda i: (i, 0, 0))
     trip_block = pl.BlockSpec((tt, wide), lambda i: (i, 0))
     n_phi, n_eta = lax.axis_size("phi"), lax.axis_size("eta")
@@ -374,16 +376,16 @@
         slot_shape, grad_shape = (slots, wide), (pack, hid)
     mda, payload, grads, bias = pl.pallas_call(
         functools.partial(main_kernel, fused),
-        grid=(steps,),
+        grid=(n_trip // tm,),
         in_specs=[
-            idx_block,
-            trip_block,
+            pl.BlockSpec((1, 1, tm), lambda i: (i, 0, 0)),
+            pl.BlockSpec((tm, wide), lambda i: (i, 0)),
             full((slots, wide)),
             full((n_in, hid)),
             full((1, hid)),
             full((hid, width)),
         ],
-        out_specs=[trip_block, full(slot_shape), full(grad_shape), full((1, hid))],
+        out_specs=[pl.BlockSpec((tm, wide), lambda i: (i, 0)), full(slot_shape), full(grad_shape), full((1, hid))],
         out_shape=[
             jax.ShapeDtypeStruct((n_trip, wide), BF16),
             jax.ShapeDtypeStruct(slot_shape, BF16),

time: 93.3 us -> 92.2 us (0.988)
  Pallas kernels: 90.1 us -> 89 us
    pallas_call x1, Pallas kernels: 33.8 us -> 32.6 us  [local(): pl.pallas_call(functools.partial(main_kernel, fused), grid=(n_trip // tm,...]
where the time goes in v4:
time: 92.2 us; the launch traced here: 91.8 us
  Pallas kernels  89 us (97%)
  other arithmetic  1.33 us (1%)
    pallas_call x1, Pallas kernels, local(): pl.pallas_call(functools.partial(main_kernel, fused), grid=(n_trip // tm,...  32.6 us
    pallas_call x1, Pallas kernels, local(): pl.pallas_call(functools.partial(scatter_kernel, n_phi, n_eta), grid=(ste...  29.4 us
    pallas_call x1, Pallas kernels, local(): pl.pallas_call(functools.partial(near_kernel, n_phi, n_eta), grid=(steps,...  21.7 us
    pallas_call x1, Pallas kernels, local(): pl.pallas_call(final_kernel, grid=(n_edges // et,), in_specs=[full((1, sl...  5.14 us

profile of v4, /device:TPU:0, one launch (start us, length us, event | category | flops | bytes accessed | tf_op | source)
XLA Modules:
  0.0 91.8 jit_solution(18388479611915231751)
XLA Ops:
  0.6 0.8 squeeze.3
  1.4 0.7 iota_compare_fusion
  2.2 0.1 lt.29
  2.2 0.6 broadcast_select_fusion.rows_ref
  2.8 21.7 %near_rows.1 = (bf16[8192,256]{1,0:T(8,128)(2,1)}, bf16[32,32,256]{2,1,0:T(8,128)(2,1)}) custom-call(s32[8,1,1024]{2,1,0:T(1,128)} %bitcast.8, s32[1,1024]{1,0:T(1,128)} %broadcast_select_fusion.rows_ref, bf16[2048,128]{1,0:T(8,128)(2,1)} %edges_ref.3, bf16[2048,128]{1,0:T(8,128)(2,1)} %cot_ref.3), custom_call_target="tpu_custom_call" | custom-call | tf_op jit(solution)/shard_map/near_rows/pallas_call | solution.py:357
  24.6 32.6 %triplets.1 = (bf16[8192,256]{1,0:T(8,128)(2,1)}, bf16[32,48,256]{2,1,0:T(8,128)(2,1)}, bf16[8,256]{1,0:T(8,128)(2,1)}, f32[1,256]{1,0:T(1,128)}) custom-call(s32[16,1,512]{2,1,0:T(1,128)} %bitcast.12, bf16[8192,256]{1,0:T(8,128)(2,1)} %get-tuple-element.19.near_ref, bf16[1024,256]{1,0:T(8,128)(2,1)} %bitcast.11, bf16[384,256]{1,0:T(8,128)(2,1)} %w1_ref.1, ...), custom_call_target="tpu_custom_call" | custom-call | flops 9663676416 | bytes 16777216 | tf_op jit(solution)/shard_map/triplets/pallas_call | solution.py:377
  57.2 29.4 %near_sum.1 = (f32[2048,256]{1,0:T(8,128)}, bf16[32,32,256]{2,1,0:T(8,128)(2,1)}, bf16[32,16,256]{2,1,0:T(8,128)(2,1)}, f32[32,1,256]{2,1,0:T(1,128)}) custom-call(s32[8,1,1024]{2,1,0:T(1,128)} %bitcast.9, bf16[8192,256]{1,0:T(8,128)(2,1)} %get-tuple-element.21.mda_ref, bf16[32,48,256]{2,1,0:T(8,128)(2,1)} %get-tuple-element.22.pay_ref, ...), custom_call_target="tpu_custom_call" | custom-call | tf_op jit(solution)/shard_map/near_sum/pallas_call | solution.py:412
  86.7 5.1 %add_up.1 = (bf16[2048,128]{1,0:T(8,128)(2,1)}, bf16[2048,128]{1,0:T(8,128)(2,1)}, f32[384,256]{1,0:T(8,128)}, f32[256,128]{1,0:T(8,128)}, f32[1,256]{1,0:T(1,128)}) custom-call(s32[1,1024]{1,0:T(1,128)} %broadcast_select_fusion.rows_ref, bf16[32,32,256]{2,1,0:T(8,128)(2,1)} %get-tuple-element.24.back_ref, f32[2048,256]{1,0:T(8,128)} %get-tuple-element.25.local_ref, ...), custom_call_target="tpu_custom_call" | custom-call | tf_op jit(solution)/shard_map/add_up/pallas_call | solution.py:442
